TPU v7x, 128 devices: a whole 4x4x4 slice. The times are simulated.
128 devices in a mesh: tiles: 128 (over y, z, x, core).
Axes of the slice: x: 4, y: 4, z: 4, core: 2. Of those that a mesh axis runs over, the one named last changes fastest.
Arguments:
- mask_param: float32 [128, 512, 512], P('tiles'), may hold values from -6 to 6
- target: bfloat16 [128, 512, 512], P('tiles'), may hold values from 0 to 1
- counts: int32 [128, 4], replicated, may hold values from 1 to 4, as said below
- kernels: float32 [4, 12, 64, 128], replicated, may hold values from -4.25 to 4.25
- weights: float32 [4, 12], replicated, may hold values from 0.1 to 1
- thresholds: float32 [4], replicated, may hold values from 0.3 to 0.6
Outputs:
- mask_out: float32 [128, 512, 512], P('tiles')
- gradient: float32 [128, 512, 512], P('tiles')
Inputs may be any that keep to these rules, and one draw needn't show every extreme that they name: `counts`: blocks 0 to 63 have 2 to 4 conditions on each tile, the other blocks one condition on each tile; in every draw some block among the first 64 has 4 conditions on all its tiles.
All inputs are finite; a program needn't handle non-finite values.
Results may differ from a plain program's by a relative error of at most 0.0095.
Values may be sent and summed in bfloat16 or wider, within the bound.
A program may use at most 64 MiB of HBM per device.

v0:
```python
import jax
import jax.numpy as jnp
from jax import lax
from jax.sharding import PartitionSpec as P

TILE = 256
HALO = 32
KF = 64
DEV_COLS = 8


STEEPNESS = 8.0
STEP_SIZE = 0.25


def from_behind(value, axis, steps):
    count = lax.axis_size(axis)
    initial, last = (max(0, -steps), min(count, count - steps))
    return lax.ppermute(value, axis, [(source, source + steps) for source in range(initial, last)])


def from_behind_2(array, axis, by):
    count = lax.axis_size(axis)
    return lax.ppermute(array, axis, [(i, (i + by) % count) for i in range(count)])


def make_tables(tile_px, margin, freq_count):
    padded = tile_px + 2 * margin
    offsets = jnp.arange(freq_count, dtype=jnp.float32) - freq_count // 2
    pixels = jnp.arange(padded, dtype=jnp.float32)
    angles = 2.0 * jnp.pi * offsets[:, None] * pixels[None, :] / padded
    forward_tab = jnp.concatenate([jnp.cos(angles), jnp.sin(angles)], 0).astype(jnp.bfloat16)
    inner_px = jnp.arange(tile_px, dtype=jnp.float32) + margin
    inner_angles = 2.0 * jnp.pi * inner_px[:, None] * offsets[None, :] / padded
    inverse_tab = jnp.stack([jnp.cos(inner_angles), jnp.sin(inner_angles)]).astype(jnp.bfloat16)
    return (forward_tab, inverse_tab)


def spectra_of(windows, forward_tab):
    freq_count = forward_tab.shape[0] // 2
    halves = jnp.einsum(
        "npx,gx->npg", windows, forward_tab, preferred_element_type=jnp.float32
    ).astype(jnp.bfloat16)
    products = jnp.einsum("hp,npg->nhg", forward_tab, halves, preferred_element_type=jnp.float32)
    real_part = products[:, :freq_count, :freq_count] - products[:, freq_count:, freq_count:]
    imag_part = -(products[:, :freq_count, freq_count:] + products[:, freq_count:, :freq_count])
    return jnp.concatenate([real_part, imag_part], 2)


def windows_of(grad_spec, forward_tab):
    freq_count = forward_tab.shape[0] // 2
    real_part = grad_spec[:, :, :freq_count]
    imag_part = grad_spec[:, :, freq_count:]
    top_rows = jnp.concatenate([real_part, -imag_part], 2)
    low_rows = jnp.concatenate([-imag_part, -real_part], 2)
    grad_whole = jnp.concatenate([top_rows, low_rows], 1)
    grad_halves = jnp.einsum(
        "hp,nhg->npg", forward_tab, grad_whole, preferred_element_type=jnp.float32
    ).astype(jnp.bfloat16)
    return jnp.einsum("npg,gx->npx", grad_halves, forward_tab, preferred_element_type=jnp.float32)


def unit_gradient(spectrum, kern_pair, weight_row, threshold, target_tile, inverse_tab, norm_scale):
    freq_count = spectrum.shape[0]
    spec_re = spectrum[:, :freq_count].astype(jnp.float32)
    spec_im = spectrum[:, freq_count:].astype(jnp.float32)
    kern_re = kern_pair[:, :, :freq_count]
    kern_im = kern_pair[:, :, freq_count:]
    mixed_spec = jnp.stack(
        [kern_re * spec_re - kern_im * spec_im, kern_re * spec_im + kern_im * spec_re], 1
    ).astype(jnp.bfloat16)
    row_prod = jnp.einsum(
        "kafm,bym->kafby", mixed_spec, inverse_tab, preferred_element_type=jnp.float32
    )
    row_half = jnp.stack(
        [row_prod[:, 0, :, 0] - row_prod[:, 1, :, 1], row_prod[:, 0, :, 1] + row_prod[:, 1, :, 0]],
        1,
    ).astype(jnp.bfloat16)
    field_parts = (
        jnp.einsum("bxf,kafy->kbaxy", inverse_tab, row_half, preferred_element_type=jnp.float32)
        * norm_scale
    )
    field_re = field_parts[:, 0, 0] - field_parts[:, 1, 1]
    field_im = field_parts[:, 0, 1] + field_parts[:, 1, 0]
    intensity = jnp.sum(weight_row[:, None, None] * (field_re * field_re + field_im * field_im), 0)
    resist = jax.nn.sigmoid(STEEPNESS * (intensity - threshold))
    grad_int = (
        2.0 * (resist - target_tile.astype(jnp.float32)) * STEEPNESS * resist * (1.0 - resist)
    )
    scaled = 2.0 * weight_row[:, None, None] * grad_int[None]
    grad_field = jnp.stack([scaled * field_re, scaled * field_im], 1).astype(jnp.bfloat16)
    grad_prod = (
        jnp.einsum("bxf,kaxy->kbafy", inverse_tab, grad_field, preferred_element_type=jnp.float32)
        * norm_scale
    )
    grad_half = jnp.stack(
        [grad_prod[:, 0, 0] + grad_prod[:, 1, 1], grad_prod[:, 0, 1] - grad_prod[:, 1, 0]], 1
    ).astype(jnp.bfloat16)
    grad_mix = jnp.einsum(
        "kafy,bym->kabfm", grad_half, inverse_tab, preferred_element_type=jnp.float32
    )
    grad_re = grad_mix[:, 0, 0] + grad_mix[:, 1, 1]
    grad_im = grad_mix[:, 1, 0] - grad_mix[:, 0, 1]
    out_re = jnp.sum(kern_re * grad_re + kern_im * grad_im, 0)
    out_im = jnp.sum(kern_re * grad_im - kern_im * grad_re, 0)
    return jnp.concatenate([out_re, out_im], 1)


def from_neighbour(sent_piece, shift_by):
    return from_behind(sent_piece.astype(jnp.bfloat16), "tiles", shift_by).astype(sent_piece.dtype)


def to_neighbour(sent_piece, shift_by):
    return from_behind(sent_piece.astype(jnp.bfloat16), "tiles", shift_by).astype(sent_piece.dtype)


def frame_direct(centre, margin, my_row, my_col, grid_rows, grid_cols):
    ranges = {-1: slice(-margin, None), 0: slice(None), 1: slice(0, margin)}
    strips = []
    for row_step in (-1, 0, 1):
        pieces_row = []
        for col_step in (-1, 0, 1):
            if row_step == 0 and col_step == 0:
                pieces_row.append(centre)
            else:
                sent_piece = centre[ranges[row_step], ranges[col_step]]
                arrived = from_neighbour(sent_piece, -(row_step * grid_cols + col_step))
                usable = (
                    (my_row + row_step >= 0)
                    & (my_row + row_step < grid_rows)
                    & (my_col + col_step >= 0)
                    & (my_col + col_step < grid_cols)
                )
                pieces_row.append(jnp.where(usable, arrived, 0.0))
        strips.append(jnp.concatenate(pieces_row, 1))
    return jnp.concatenate(strips, 0)


def fold_direct(canvas, margin, my_row, my_col, grid_rows, grid_cols):
    rows_in = canvas.shape[0] - 2 * margin
    cols_in = canvas.shape[1] - 2 * margin
    row_source = {
        -1: slice(0, margin),
        0: slice(margin, margin + rows_in),
        1: slice(margin + rows_in, None),
    }
    col_source = {
        -1: slice(0, margin),
        0: slice(margin, margin + cols_in),
        1: slice(margin + cols_in, None),
    }
    row_target = {1: slice(0, margin), 0: slice(None), -1: slice(rows_in - margin, rows_in)}
    col_target = {1: slice(0, margin), 0: slice(None), -1: slice(cols_in - margin, cols_in)}
    centre = canvas[margin : margin + rows_in, margin : margin + cols_in]
    for row_step in (-1, 0, 1):
        for col_step in (-1, 0, 1):
            if row_step != 0 or col_step != 0:
                sent_piece = canvas[row_source[row_step], col_source[col_step]]
                arrived = to_neighbour(sent_piece, row_step * grid_cols + col_step)
                usable = (
                    (my_row - row_step >= 0)
                    & (my_row - row_step < grid_rows)
                    & (my_col - col_step >= 0)
                    & (my_col - col_step < grid_cols)
                )
                centre = centre.at[row_target[row_step], col_target[col_step]].add(
                    jnp.where(usable, arrived, 0.0)
                )
    return centre


def shards(mask_param, target, counts, kernels, weights, thresholds):
    levels = mask_param[0]
    block_rows, block_cols = levels.shape
    tile_px = TILE
    margin = HALO
    freq_count = KF
    padded = tile_px + 2 * margin
    tile_rows = block_rows // tile_px
    tile_cols = block_cols // tile_px
    per_block = tile_rows * tile_cols
    cond_count = kernels.shape[0]
    norm_scale = 1.0 / (padded * freq_count)
    forward_tab, inverse_tab = make_tables(tile_px, margin, freq_count)
    devices = lax.axis_size("tiles")
    half_axis = devices // 2
    my_index = lax.axis_index("tiles")
    grid_cols = DEV_COLS
    grid_rows = devices // grid_cols
    my_col = my_index % grid_cols
    my_row = my_index // grid_cols
    own_counts = lax.dynamic_index_in_dim(counts, my_index, 0, keepdims=False)
    targets = (
        target[0]
        .reshape(tile_rows, tile_px, tile_cols, tile_px)
        .transpose(0, 2, 1, 3)
        .reshape(per_block, tile_px, tile_px)
    )
    partner_targets = from_behind_2(targets, "tiles", half_axis)
    is_first = my_index < half_axis
    partner_counts = lax.dynamic_index_in_dim(
        counts, (my_index + half_axis) % devices, 0, keepdims=False
    )
    pair_targets = jnp.where(
        is_first,
        jnp.concatenate([targets, partner_targets], 0),
        jnp.concatenate([partner_targets, targets], 0),
    )
    pair_counts = jnp.where(
        is_first,
        jnp.concatenate([own_counts, partner_counts]),
        jnp.concatenate([partner_counts, own_counts]),
    )
    slot_count = 5 * per_block // 2
    unit_ids = jnp.arange(2 * per_block * cond_count, dtype=jnp.int32)
    unit_live = unit_ids % cond_count < jnp.repeat(pair_counts, cond_count)
    unit_rank = jnp.cumsum(unit_live.astype(jnp.int32)) - 1
    first_rank = jnp.where(is_first, slot_count, 0)
    wanted = first_rank + jnp.arange(slot_count, dtype=jnp.int32)
    chosen = unit_live[None, :] & (unit_rank[None, :] == wanted[:, None])
    slot_live = jnp.any(chosen, 1)
    slot_unit = jnp.sum(jnp.where(chosen, unit_ids[None, :], 0), 1)
    slot_tile = slot_unit // cond_count
    slot_cond = slot_unit % cond_count
    tile_onehot = (
        (slot_tile[:, None] == jnp.arange(2 * per_block, dtype=jnp.int32)[None, :])
        & slot_live[:, None]
    ).astype(jnp.float32)
    opening = jax.nn.sigmoid(levels)
    transmit = 2.0 * opening - 1.0
    framed = frame_direct(transmit, margin, my_row, my_col, grid_rows, grid_cols)
    windows = jnp.stack(
        [
            framed[
                row_tile * tile_px : row_tile * tile_px + padded,
                col_tile * tile_px : col_tile * tile_px + padded,
            ]
            for row_tile in range(tile_rows)
            for col_tile in range(tile_cols)
        ]
    ).astype(jnp.bfloat16)
    spectra = spectra_of(windows, forward_tab).astype(jnp.bfloat16)
    partner_spectra = from_behind_2(spectra, "tiles", half_axis)
    pair_spectra = jnp.where(
        is_first,
        jnp.concatenate([spectra, partner_spectra], 0),
        jnp.concatenate([partner_spectra, spectra], 0),
    )

    def run_pair_slot(slot_data):
        tile_at, cond_at, live_at = slot_data
        unit_term = unit_gradient(
            pair_spectra[tile_at],
            kernels[cond_at],
            weights[cond_at],
            thresholds[cond_at],
            pair_targets[tile_at],
            inverse_tab,
            norm_scale,
        )
        return jnp.where(live_at, unit_term, 0.0)

    slot_terms = lax.map(run_pair_slot, (slot_tile, slot_cond, slot_live))
    pair_grads = jnp.einsum("jt,jfg->tfg", tile_onehot, slot_terms, precision=lax.Precision.HIGHEST)
    own_part = jnp.where(is_first, pair_grads[:per_block], pair_grads[per_block:])
    other_part = jnp.where(is_first, pair_grads[per_block:], pair_grads[:per_block])
    grad_spec = own_part + from_behind_2(
        other_part.astype(jnp.bfloat16), "tiles", half_axis
    ).astype(other_part.dtype)
    grad_windows = windows_of(grad_spec.astype(jnp.bfloat16), forward_tab)
    canvas = jnp.zeros((block_rows + 2 * margin, block_cols + 2 * margin), jnp.float32)
    for row_tile in range(tile_rows):
        for col_tile in range(tile_cols):
            canvas = canvas.at[
                row_tile * tile_px : row_tile * tile_px + padded,
                col_tile * tile_px : col_tile * tile_px + padded,
            ].add(grad_windows[row_tile * tile_cols + col_tile])
    grad_inner = fold_direct(canvas, margin, my_row, my_col, grid_rows, grid_cols)
    gradient = grad_inner * 2.0 * opening * (1.0 - opening)
    levels = levels - STEP_SIZE * gradient
    return (levels[None], gradient[None])


def solution(mesh):
    placed = (P("tiles", None, None), P("tiles", None, None), P(), P(), P(), P())
    return jax.shard_map(
        shards,
        mesh=mesh,
        in_specs=placed,
        out_specs=(P("tiles", None, None), P("tiles", None, None)),
        check_vma=False,
    )
```

profile of v0, /device:TPU:7, one launch (start us, length us, event | category | flops | bytes accessed | tf_op | source)
XLA Modules:
  0.0 308.7 jit_solution(13332083495277189464)
XLA Ops:
  0.6 1.6 multiply_add_fusion
  2.3 2.6 collective-permute-start.4
  4.9 5.1 %collective-permute-start.3 = (bf16[512,32]{1,0:T(8,128)(2,1)S(1)}, bf16[512,32]{1,0:T(8,128)(2,1)S(1)}, u32[]{:S(2)}, u32[]{:S(2)}) collective-permute-start(bf16[512,32]{1,0:T(8,128)(2,1)S(1)} %get-tuple-element.341), channel_id=1, source_target_pairs={{0,1},{1,2},{2,3},{3,4},{4,5},{5,6},{6,7},{7,8},{8,9},{9,10},{10,1... | collective-permute-start | bytes 98312 | tf_op jit(solution)/shard_map/ppermute | solution.py:19
  10.0 3.5 %collective-permute-start.1 = (bf16[32,512]{1,0:T(8,128)(2,1)S(1)}, bf16[32,512]{1,0:T(8,128)(2,1)S(1)}, u32[]{:S(2)}, u32[]{:S(2)}) collective-permute-start(bf16[32,512]{1,0:T(8,128)(2,1)S(1)} %get-tuple-element.339), channel_id=1, source_target_pairs={{0,8},{1,9},{2,10},{3,11},{4,12},{5,13},{6,14},{7,15},{8,16},{9,17... | collective-permute-start | bytes 98312 | tf_op jit(solution)/shard_map/ppermute | solution.py:19
  13.7 1.9 collective-permute-start.2
  15.6 10.0 %collective-permute-start = (bf16[32,32]{1,0:T(8,128)(2,1)S(1)}, bf16[32,32]{1,0:T(8,128)(2,1)S(1)}, u32[]{:S(2)}, u32[]{:S(2)}) collective-permute-start(bf16[32,32]{1,0:T(8,128)(2,1)S(1)} %get-tuple-element.335), channel_id=1, source_target_pairs={{0,9},{1,10},{2,11},{3,12},{4,13},{5,14},{6,15},{7,16},{8,17},{9,1... | collective-permute-start | bytes 6152 | tf_op jit(solution)/shard_map/ppermute | solution.py:19
  35.7 7.3 %collective-permute-done.7 = bf16[32,32]{1,0:T(8,128)(2,1)S(1)} collective-permute-done((bf16[32,32]{1,0:T(8,128)(2,1)S(1)}, bf16[32,32]{1,0:T(8,128)(2,1)S(1)}, u32[]{:S(2)}, u32[]{:S(2)}) %collective-permute-start.7) | collective-permute-done | bytes 2080 | tf_op jit(solution)/shard_map/ppermute | solution.py:19
  43.0 1.9 collective-permute-start.5
  44.9 3.0 collective-permute-done.5
  47.9 3.5 %collective-permute-start.9 = (bf16[4,256,256]{1,2,0:T(8,128)(2,1)S(1)}, bf16[4,256,256]{1,2,0:T(8,128)(2,1)S(1)}, u32[]{:S(2)}, u32[]{:S(2)}) collective-permute-start(bf16[4,256,256]{1,2,0:T(8,128)(2,1)S(1)} %bitcast.301), channel_id=1, source_target_pairs={{0,64},{1,65},{2,66},{3,67},{4,68},{5,69},{6,70},{7,71},{8,72},{9,... | collective-permute-start | bytes 1572872 | tf_op jit(solution)/shard_map/ppermute | solution.py:24
  52.9 1.9 fusion.42
  55.3 9.0 %collective-permute-done.8 = bf16[4,64,128]{2,1,0:T(8,128)(2,1)S(1)} collective-permute-done((bf16[4,64,128]{2,1,0:T(8,128)(2,1)S(1)}, bf16[4,64,128]{2,1,0:T(8,128)(2,1)S(1)}, u32[]{:S(2)}, u32[]{:S(2)}) %collective-permute-start.8) | collective-permute-done | bytes 65568 | tf_op jit(solution)/shard_map/ppermute | solution.py:24
  64.7 175.6 %while.24 = (s32[]{:T(128)}, f32[10,64,128]{2,0,1:T(8,128)S(1)}, pred[10]{0:T(512)(128)(4,1)S(1)}, s32[10]{0:T(128)S(1)}, f32[4,12,64,128]{3,2,1,0:T(8,128)}, /*...) while((s32[]{:T(128)}, f32[10,64,128]{2,0,1:T(8,128)S(1)}, ...), condition=%wide.region_7.8_spmd, body=%wide.region_3.7_spmd.sunk | while | flops 1028636672 | bytes 65028612 | solution.py:263
  71.9 1.8 multiply_bitcast_fusion.4
  77.1 1.5 fusion.127
  89.4 1.8 multiply_bitcast_fusion.4
  94.6 1.5 fusion.127
  107.0 1.8 multiply_bitcast_fusion.4
  112.2 1.5 fusion.127
  124.6 1.8 multiply_bitcast_fusion.4
  129.7 1.5 fusion.127
  142.1 1.8 multiply_bitcast_fusion.4
  147.3 1.5 fusion.127
  159.7 1.8 multiply_bitcast_fusion.4
  164.9 1.5 fusion.127
  177.2 1.8 multiply_bitcast_fusion.4
  182.4 1.5 fusion.127
  194.8 1.8 multiply_bitcast_fusion.4
  212.4 1.8 multiply_bitcast_fusion.4
  217.5 1.5 fusion.127
  229.9 1.8 multiply_bitcast_fusion.4
  235.1 1.5 fusion.127
  240.7 3.3 %collective-permute-start.10 = (bf16[4,64,128]{2,0,1:T(4,128)(2,1)S(1)}, bf16[4,64,128]{2,0,1:T(4,128)(2,1)S(1)}, u32[]{:S(2)}, u32[]{:S(2)}) collective-permute-start(bf16[4,64,128]{2,0,1:T(4,128)(2,1)S(1)} %select_convert_fusion), channel_id=1, source_target_pairs={{0,64},{1,65},{2,66},{3,67},{4,68},{5,69},{6,70},{7,71},{8,72},{9,... | collective-permute-start | bytes 196616 | tf_op jit(solution)/shard_map/ppermute | solution.py:24
  244.6 1.6 collective-permute-done.10
  246.6 1.6 fusion.41
  248.3 2.9 add_select_fusion
  251.2 5.3 %scatter-add.41 = f32[576,576]{1,0:T(8,128)S(1)} dynamic-update-slice(f32[576,576]{1,0:T(8,128)S(1)} %scatter-add.40, f32[320,320]{1,0:T(8,128)} %add_select_fusion, s32[]{:T(128)} %bitcast.49, s32[]{:T(128)} %bitcast.50) | dynamic-update-slice | bytes 819204 | tf_op jit(solution)/shard_map/scatter-add | solution.py:277
  257.4 4.3 %scatter-add.44 = f32[576,576]{1,0:T(8,128)S(1)} dynamic-update-slice(f32[576,576]{1,0:T(8,128)S(1)} %scatter-add.41, f32[320,320]{1,0:T(8,128)} %fusion.62, s32[]{:T(128)} %constant.480.clone.1, s32[]{:T(128)} %constant.460.clone.1) | dynamic-update-slice | bytes 819204 | tf_op jit(solution)/shard_map/scatter-add | solution.py:277
  265.2 1.9 collective-permute-start.13
  267.1 2.1 collective-permute-start.14
  269.2 5.6 %collective-permute-start.15 = (bf16[512,32]{1,0:T(8,128)(2,1)S(1)}, bf16[512,32]{1,0:T(8,128)(2,1)S(1)}, u32[]{:S(2)}, u32[]{:S(2)}) collective-permute-start(bf16[512,32]{1,0:T(8,128)(2,1)S(1)} %get-tuple-element.333), channel_id=1, source_target_pairs={{0,1},{1,2},{2,3},{3,4},{4,5},{5,6},{6,7},{7,8},{8,9},{9,10},{10,1... | collective-permute-start | bytes 98312 | tf_op jit(solution)/shard_map/ppermute | solution.py:19
  274.8 1.9 collective-permute-start.16
  277.6 5.3 %collective-permute-start.17 = (bf16[32,512]{1,0:T(8,128)(2,1)S(1)}, bf16[32,512]{1,0:T(8,128)(2,1)S(1)}, u32[]{:S(2)}, u32[]{:S(2)}) collective-permute-start(bf16[32,512]{1,0:T(8,128)(2,1)S(1)} %get-tuple-element.328), channel_id=1, source_target_pairs={{0,8},{1,9},{2,10},{3,11},{4,12},{5,13},{6,14},{7,15},{8,16},{9,17... | collective-permute-start | bytes 98312 | tf_op jit(solution)/shard_map/ppermute | solution.py:19
  283.0 12.7 %collective-permute-start.18 = (bf16[32,32]{1,0:T(8,128)(2,1)S(1)}, bf16[32,32]{1,0:T(8,128)(2,1)S(1)}, u32[]{:S(2)}, u32[]{:S(2)}) collective-permute-start(bf16[32,32]{1,0:T(8,128)(2,1)S(1)} %slice.763), channel_id=1, source_target_pairs={{0,9},{1,10},{2,11},{3,12},{4,13},{5,14},{6,15},{7,16},{8,17},{9,1... | collective-permute-start | bytes 6152 | tf_op jit(solution)/shard_map/ppermute | solution.py:19
  298.6 1.9 scatter-add.54
  300.6 2.0 add_select_fusion.2
  302.5 2.2 scatter-add.55
  305.7 3.0 fusion.67
  (317 shorter events, 126.4 us)
Async XLA Ops:
  0.6 29.9 %copy-start.1 = (bf16[1,512,512]{2,1,0:T(8,128)(2,1)S(1)}, bf16[1,512,512]{2,1,0:T(8,128)(2,1)}, u32[]{:S(2)}) copy-start(bf16[1,512,512]{2,1,0:T(8,128)(2,1)} %param.33) | copy-start | bytes 1572868
  2.3 49.2 %collective-permute-start.4 = (bf16[512,32]{1,0:T(8,128)(2,1)S(1)}, bf16[512,32]{1,0:T(8,128)(2,1)S(1)}, u32[]{:S(2)}, u32[]{:S(2)}) collective-permute-start(bf16[512,32]{1,0:T(8,128)(2,1)S(1)} %get-tuple-element.342), channel_id=1, source_target_pairs={{1,0},{2,1},{3,2},{4,3},{5,4},{6,5},{7,6},{8,7},{9,8},{10,9},{11,1... | collective-permute-start | bytes 98312 | tf_op jit(solution)/shard_map/ppermute | solution.py:19
  4.9 46.6 %collective-permute-start.3 = (bf16[512,32]{1,0:T(8,128)(2,1)S(1)}, bf16[512,32]{1,0:T(8,128)(2,1)S(1)}, u32[]{:S(2)}, u32[]{:S(2)}) collective-permute-start(bf16[512,32]{1,0:T(8,128)(2,1)S(1)} %get-tuple-element.341), channel_id=1, source_target_pairs={{0,1},{1,2},{2,3},{3,4},{4,5},{5,6},{6,7},{7,8},{8,9},{9,10},{10,1... | collective-permute-start | bytes 98312 | tf_op jit(solution)/shard_map/ppermute | solution.py:19
  10.0 41.6 %collective-permute-start.1 = (bf16[32,512]{1,0:T(8,128)(2,1)S(1)}, bf16[32,512]{1,0:T(8,128)(2,1)S(1)}, u32[]{:S(2)}, u32[]{:S(2)}) collective-permute-start(bf16[32,512]{1,0:T(8,128)(2,1)S(1)} %get-tuple-element.339), channel_id=1, source_target_pairs={{0,8},{1,9},{2,10},{3,11},{4,12},{5,13},{6,14},{7,15},{8,16},{9,17... | collective-permute-start | bytes 98312 | tf_op jit(solution)/shard_map/ppermute | solution.py:19
  13.7 19.4 %collective-permute-start.2 = (bf16[32,32]{1,0:T(8,128)(2,1)S(1)}, bf16[32,32]{1,0:T(8,128)(2,1)S(1)}, u32[]{:S(2)}, u32[]{:S(2)}) collective-permute-start(bf16[32,32]{1,0:T(8,128)(2,1)S(1)} %get-tuple-element.337), channel_id=1, source_target_pairs={{0,7},{1,8},{2,9},{3,10},{4,11},{5,12},{6,13},{7,14},{8,15},{9,16}... | collective-permute-start | bytes 6152 | tf_op jit(solution)/shard_map/ppermute | solution.py:19
  15.6 18.8 %collective-permute-start = (bf16[32,32]{1,0:T(8,128)(2,1)S(1)}, bf16[32,32]{1,0:T(8,128)(2,1)S(1)}, u32[]{:S(2)}, u32[]{:S(2)}) collective-permute-start(bf16[32,32]{1,0:T(8,128)(2,1)S(1)} %get-tuple-element.335), channel_id=1, source_target_pairs={{0,9},{1,10},{2,11},{3,12},{4,13},{5,14},{6,15},{7,16},{8,17},{9,1... | collective-permute-start | bytes 6152 | tf_op jit(solution)/shard_map/ppermute | solution.py:19
  28.8 35.9 %copy-start = (bf16[64,320]{0,1:T(8,128)(2,1)}, bf16[64,320]{0,1:T(8,128)(2,1)S(1)}, u32[]{:S(2)}) copy-start(bf16[64,320]{0,1:T(8,128)(2,1)S(1)} %get-tuple-element.355) | copy-start | bytes 122884
  33.1 18.8 %collective-permute-start.6 = (bf16[32,512]{1,0:T(8,128)(2,1)S(1)}, bf16[32,512]{1,0:T(8,128)(2,1)S(1)}, u32[]{:S(2)}, u32[]{:S(2)}) collective-permute-start(bf16[32,512]{1,0:T(8,128)(2,1)S(1)} %get-tuple-element.340), channel_id=1, source_target_pairs={{8,0},{9,1},{10,2},{11,3},{12,4},{13,5},{14,6},{15,7},{16,8},{17,9... | collective-permute-start | bytes 98312 | tf_op jit(solution)/shard_map/ppermute | solution.py:19
  34.4 8.6 %collective-permute-start.7 = (bf16[32,32]{1,0:T(8,128)(2,1)S(1)}, bf16[32,32]{1,0:T(8,128)(2,1)S(1)}, u32[]{:S(2)}, u32[]{:S(2)}) collective-permute-start(bf16[32,32]{1,0:T(8,128)(2,1)S(1)} %get-tuple-element.338), channel_id=1, source_target_pairs={{9,0},{10,1},{11,2},{12,3},{13,4},{14,5},{15,6},{16,7},{17,8},{18,... | collective-permute-start | bytes 6152 | tf_op jit(solution)/shard_map/ppermute | solution.py:19
  43.0 5.0 %collective-permute-start.5 = (bf16[32,32]{1,0:T(8,128)(2,1)S(1)}, bf16[32,32]{1,0:T(8,128)(2,1)S(1)}, u32[]{:S(2)}, u32[]{:S(2)}) collective-permute-start(bf16[32,32]{1,0:T(8,128)(2,1)S(1)} %get-tuple-element.336), channel_id=1, source_target_pairs={{7,0},{8,1},{9,2},{10,3},{11,4},{12,5},{13,6},{14,7},{15,8},{16,9}... | collective-permute-start | bytes 6152 | tf_op jit(solution)/shard_map/ppermute | solution.py:19
  47.9 16.5 %collective-permute-start.9 = (bf16[4,256,256]{1,2,0:T(8,128)(2,1)S(1)}, bf16[4,256,256]{1,2,0:T(8,128)(2,1)S(1)}, u32[]{:S(2)}, u32[]{:S(2)}) collective-permute-start(bf16[4,256,256]{1,2,0:T(8,128)(2,1)S(1)} %bitcast.301), channel_id=1, source_target_pairs={{0,64},{1,65},{2,66},{3,67},{4,68},{5,69},{6,70},{7,71},{8,72},{9,... | collective-permute-start | bytes 1572872 | tf_op jit(solution)/shard_map/ppermute | solution.py:24
  52.9 11.7 %copy-start.2 = (pred[10]{0:T(512)(128)(4,1)S(1)}, pred[10]{0:T(512)(128)(4,1)}, u32[]{:S(2)}) copy-start(pred[10]{0:T(512)(128)(4,1)} %fusion.77) | copy-start | bytes 34
  52.9 11.7 %copy-start.3 = (s32[10]{0:T(128)S(1)}, s32[10]{0:T(128)}, u32[]{:S(2)}) copy-start(s32[10]{0:T(128)} %get-tuple-element.451) | copy-start | bytes 124
  52.9 11.8 %copy-start.4 = (f32[4]{0:T(128)S(1)}, f32[4]{0:T(128)}, u32[]{:S(2)}) copy-start(f32[4]{0:T(128)} %param.37) | copy-start | bytes 52
  52.9 11.8 %copy-start.5 = (s32[10]{0:T(128)S(1)}, s32[10]{0:T(128)}, u32[]{:S(2)}) copy-start(s32[10]{0:T(128)} %get-tuple-element.448) | copy-start | bytes 124
  55.1 9.3 %collective-permute-start.8 = (bf16[4,64,128]{2,1,0:T(8,128)(2,1)S(1)}, bf16[4,64,128]{2,1,0:T(8,128)(2,1)S(1)}, u32[]{:S(2)}, u32[]{:S(2)}) collective-permute-start(bf16[4,64,128]{2,1,0:T(8,128)(2,1)S(1)} %pad_maximum_fusion.8), channel_id=1, source_target_pairs={{0,64},{1,65},{2,66},{3,67},{4,68},{5,69},{6,70},{7,71},{8,72},{9,... | collective-permute-start | bytes 196616 | tf_op jit(solution)/shard_map/ppermute | solution.py:24
  240.7 5.5 %collective-permute-start.10 = (bf16[4,64,128]{2,0,1:T(4,128)(2,1)S(1)}, bf16[4,64,128]{2,0,1:T(4,128)(2,1)S(1)}, u32[]{:S(2)}, u32[]{:S(2)}) collective-permute-start(bf16[4,64,128]{2,0,1:T(4,128)(2,1)S(1)} %select_convert_fusion), channel_id=1, source_target_pairs={{0,64},{1,65},{2,66},{3,67},{4,68},{5,69},{6,70},{7,71},{8,72},{9,... | collective-permute-start | bytes 196616 | tf_op jit(solution)/shard_map/ppermute | solution.py:24
  262.1 12.7 %collective-permute-start.11 = (bf16[32,32]{1,0:T(8,128)(2,1)S(1)}, bf16[32,32]{1,0:T(8,128)(2,1)S(1)}, u32[]{:S(2)}, u32[]{:S(2)}) collective-permute-start(bf16[32,32]{1,0:T(8,128)(2,1)S(1)} %get-tuple-element.332), channel_id=1, source_target_pairs={{9,0},{10,1},{11,2},{12,3},{13,4},{14,5},{15,6},{16,7},{17,8},{18,... | collective-permute-start | bytes 6152 | tf_op jit(solution)/shard_map/ppermute | solution.py:19
  263.9 13.7 %collective-permute-start.12 = (bf16[32,512]{1,0:T(8,128)(2,1)S(1)}, bf16[32,512]{1,0:T(8,128)(2,1)S(1)}, u32[]{:S(2)}, u32[]{:S(2)}) collective-permute-start(bf16[32,512]{1,0:T(8,128)(2,1)S(1)} %get-tuple-element.329), channel_id=1, source_target_pairs={{8,0},{9,1},{10,2},{11,3},{12,4},{13,5},{14,6},{15,7},{16,8},{17,9... | collective-permute-start | bytes 98312 | tf_op jit(solution)/shard_map/ppermute | solution.py:19
  265.2 17.8 %collective-permute-start.13 = (bf16[32,32]{1,0:T(8,128)(2,1)S(1)}, bf16[32,32]{1,0:T(8,128)(2,1)S(1)}, u32[]{:S(2)}, u32[]{:S(2)}) collective-permute-start(bf16[32,32]{1,0:T(8,128)(2,1)S(1)} %get-tuple-element.331), channel_id=1, source_target_pairs={{7,0},{8,1},{9,2},{10,3},{11,4},{12,5},{13,6},{14,7},{15,8},{16,9}... | collective-permute-start | bytes 6152 | tf_op jit(solution)/shard_map/ppermute | solution.py:19
  267.1 29.2 %collective-permute-start.14 = (bf16[512,32]{1,0:T(8,128)(2,1)S(1)}, bf16[512,32]{1,0:T(8,128)(2,1)S(1)}, u32[]{:S(2)}, u32[]{:S(2)}) collective-permute-start(bf16[512,32]{1,0:T(8,128)(2,1)S(1)} %get-tuple-element.334), channel_id=1, source_target_pairs={{1,0},{2,1},{3,2},{4,3},{5,4},{6,5},{7,6},{8,7},{9,8},{10,9},{11,1... | collective-permute-start | bytes 98312 | tf_op jit(solution)/shard_map/ppermute | solution.py:19
  269.2 28.7 %collective-permute-start.15 = (bf16[512,32]{1,0:T(8,128)(2,1)S(1)}, bf16[512,32]{1,0:T(8,128)(2,1)S(1)}, u32[]{:S(2)}, u32[]{:S(2)}) collective-permute-start(bf16[512,32]{1,0:T(8,128)(2,1)S(1)} %get-tuple-element.333), channel_id=1, source_target_pairs={{0,1},{1,2},{2,3},{3,4},{4,5},{5,6},{6,7},{7,8},{8,9},{9,10},{10,1... | collective-permute-start | bytes 98312 | tf_op jit(solution)/shard_map/ppermute | solution.py:19
  274.8 25.8 %collective-permute-start.16 = (bf16[32,32]{1,0:T(8,128)(2,1)S(1)}, bf16[32,32]{1,0:T(8,128)(2,1)S(1)}, u32[]{:S(2)}, u32[]{:S(2)}) collective-permute-start(bf16[32,32]{1,0:T(8,128)(2,1)S(1)} %get-tuple-element.330), channel_id=1, source_target_pairs={{0,7},{1,8},{2,9},{3,10},{4,11},{5,12},{6,13},{7,14},{8,15},{9,16}... | collective-permute-start | bytes 6152 | tf_op jit(solution)/shard_map/ppermute | solution.py:19
  277.6 27.2 %collective-permute-start.17 = (bf16[32,512]{1,0:T(8,128)(2,1)S(1)}, bf16[32,512]{1,0:T(8,128)(2,1)S(1)}, u32[]{:S(2)}, u32[]{:S(2)}) collective-permute-start(bf16[32,512]{1,0:T(8,128)(2,1)S(1)} %get-tuple-element.328), channel_id=1, source_target_pairs={{0,8},{1,9},{2,10},{3,11},{4,12},{5,13},{6,14},{7,15},{8,16},{9,17... | collective-permute-start | bytes 98312 | tf_op jit(solution)/shard_map/ppermute | solution.py:19
  283.0 21.8 %collective-permute-start.18 = (bf16[32,32]{1,0:T(8,128)(2,1)S(1)}, bf16[32,32]{1,0:T(8,128)(2,1)S(1)}, u32[]{:S(2)}, u32[]{:S(2)}) collective-permute-start(bf16[32,32]{1,0:T(8,128)(2,1)S(1)} %slice.763), channel_id=1, source_target_pairs={{0,9},{1,10},{2,11},{3,12},{4,13},{5,14},{6,15},{7,16},{8,17},{9,1... | collective-permute-start | bytes 6152 | tf_op jit(solution)/shard_map/ppermute | solution.py:19
where the time goes:
time: 311 us; the launch traced here: 309 us
  other arithmetic  77.9 us (25%)
  starting transfers between devices  66.8 us (21%)
  local copies, waits for them, and re-layouts  56.9 us (18%)
  matrix products  44.6 us (14%)
  loops' own time  40 us (13%)
  waiting for transfers between devices  21 us (7%)
    ppermute x16, starting transfers between devices, from_behind(): lax.ppermute(value, axis, [(source, source + steps) for source in range(i...  59.7 us
    another operation x1, loops' own time, shards(): slot_terms = lax.map(run_pair_slot, (slot_tile, slot_cond, slot_live))  40 us
    another operation x23, other arithmetic  24 us
    dot_general x10, matrix products, unit_gradient(): jnp.einsum('bxf,kafy->kbaxy', inverse_tab, row_half, preferred_element_ty...  18.1 us
    dynamic_slice x30, local copies, waits for them, and re-layouts, shards(): slot_terms = lax.map(run_pair_slot, (slot_tile, slot_cond, slot_live))  17.7 us
    mul x20, other arithmetic, unit_gradient(): scaled = 2.0 * weight_row[:, None, None] * grad_int[None]  14.5 us
    dot_general x10, matrix products, unit_gradient(): jnp.einsum('bxf,kaxy->kbafy', inverse_tab, grad_field, preferred_element_...  13.4 us
    reduce_sum x10, other arithmetic, unit_gradient(): jnp.sum(weight_row[:, None, None] * (field_re * field_re + field_im * fie...  13.2 us
  transfers between devices with their start and end apart: 19, of which 4 were waited for; matrix products, arithmetic and copies ran while one was open for 7% of the time, Pallas kernels for 0%

commit v1 on v0

v1 whole, which is shorter than its diff:
```python
import functools

import jax
import jax.numpy as jnp
import ml_dtypes
import numpy as np
from jax import lax
from jax.experimental import pallas as pl
from jax.experimental.pallas import tpu as pltpu
from jax.sharding import PartitionSpec as P

TILE = 256
HALO = 32
KF = 64
DEV_COLS = 8
PADDED = TILE + 2 * HALO
COARSE = 2 * KF
NK = 12
CONDS = 4
STEEPNESS = 8.0
STEP_SIZE = 0.25
SCALE = 1.0 / (PADDED * KF)

F32 = jnp.float32
BF16 = jnp.bfloat16
MESH = pl.DeviceIdType.MESH
WAYS = [(dr, dc) for dr in (-1, 0, 1) for dc in (-1, 0, 1) if (dr, dc) != (0, 0)]


def bf(values):
    return np.asarray(values, np.float32).astype(ml_dtypes.bfloat16)


def edge_table():
    freq = np.arange(KF) - KF // 2
    pixels = np.arange(PADDED)
    angles = 2.0 * np.pi * freq[:, None] * pixels[None, :] / PADDED
    forward = np.concatenate([np.cos(angles), np.sin(angles)], 0)
    table = np.zeros((2 * TILE, 4 * 2 * KF))
    for slot in range(4):
        first = (slot - 1) * TILE - HALO
        for pixel in range(2 * TILE):
            if 0 <= pixel - first < PADDED:
                table[pixel, slot * 2 * KF : (slot + 1) * 2 * KF] = forward[:, pixel - first]
    return bf(table)


def unit_tables():
    freq = np.arange(KF) - KF // 2
    angles = 2.0 * np.pi * np.arange(COARSE)[:, None] * freq[None, :] / COARSE
    cos_t, sin_t = np.cos(angles), np.sin(angles)
    t1 = np.block([[cos_t.T, sin_t.T], [-sin_t.T, cos_t.T]])
    t2 = np.block([[cos_t, -sin_t], [sin_t, cos_t]])
    shift = (np.arange(TILE) + HALO)[:, None] - PADDED / COARSE * np.arange(COARSE)[None, :]
    waves = np.arange(1, COARSE // 2)
    interp = (
        1.0 + 2.0 * np.cos(2.0 * np.pi * shift[:, :, None] * waves / PADDED).sum(-1)
    ) / COARSE
    up_hi = bf(interp)
    up_lo = bf(interp - up_hi.astype(np.float64))
    return np.concatenate(
        [
            bf(t1),
            bf(t2.T),
            up_hi.T,
            np.concatenate([up_hi, up_hi], 1),
            np.concatenate([up_hi.T, up_hi.T, up_lo.T], 0),
            np.concatenate([bf(t2), bf(t1.T)], 1),
            np.concatenate([up_lo, up_hi], 1),
        ],
        0,
    )


EDGE = edge_table()
EDGE_T = np.ascontiguousarray(EDGE.T)
UNIT = unit_tables()


def dot(a, b):
    return jnp.dot(a, b, preferred_element_type=F32)


def swap_pair(v):
    return jnp.concatenate(
        [
            jnp.concatenate([v[:64, :128], v[64:, :128]], 1),
            jnp.concatenate([v[:64, 128:], v[64:, 128:]], 1),
        ],
        0,
    )


def low_half(shape):
    return lax.broadcasted_iota(jnp.int32, shape, 1) < KF


def gradient_kernel(
    counts, weights, thresholds, mask, target, kernels, edge, edge_t, unit,
    out,
    levels, pixels, halves, part, got, spec, tgt, kraw, kre, kim, fields, acc, gspec, shared, edge_v, edge_tv, unit_v,
    load_sem, send_sem, recv_sem,
):
    me = lax.axis_index("tiles")
    devices = lax.axis_size("tiles")
    quarter = devices // 4
    half = devices // 2
    my_col = me % DEV_COLS
    my_row = me // DEV_COLS
    grid_rows = devices // DEV_COLS
    heavy = me < half
    partner = me + (3 - 2 * (me // quarter)) * quarter

    def has(dr, dc):
        ok = (my_row + dr >= 0) & (my_row + dr < grid_rows)
        return ok & (my_col + dc >= 0) & (my_col + dc < DEV_COLS)

    def peer(dr, dc):
        return lax.rem(me + dr * DEV_COLS + dc + devices, devices)

    loads = [
        pltpu.make_async_copy(mask.at[0], levels, load_sem.at[0]),
        pltpu.make_async_copy(edge, edge_v, load_sem.at[1]),
        pltpu.make_async_copy(edge_t, edge_tv, load_sem.at[2]),
        pltpu.make_async_copy(kernels, kraw, load_sem.at[3]),
        pltpu.make_async_copy(unit, unit_v, load_sem.at[4]),
    ] + [
        pltpu.make_async_copy(
            target.at[0, pl.ds((k // 2) * TILE, TILE), pl.ds((k % 2) * TILE, TILE)],
            tgt.at[k],
            load_sem.at[5 + k],
        )
        for k in range(4)
    ]
    for load in loads:
        load.start()

    barrier = pltpu.get_barrier_semaphore()
    greeted = jnp.int32(1)
    for dr, dc in WAYS:
        greeted = greeted + has(dr, dc).astype(jnp.int32)

        @pl.when(has(dr, dc))
        def _():
            pl.semaphore_signal(barrier, inc=1, device_id=(peer(dr, dc),), device_id_type=MESH)

    pl.semaphore_signal(barrier, inc=1, device_id=(partner,), device_id_type=MESH)

    def remote(src, dst, number, to):
        return pltpu.make_async_remote_copy(
            src_ref=src,
            dst_ref=dst,
            send_sem=send_sem.at[number],
            recv_sem=recv_sem.at[number],
            device_id=(to,),
            device_id_type=MESH,
        )

    span = {-1: 0, 0: pl.ds(1, 2), 1: 3}
    back = {-1: 3, 0: pl.ds(1, 2), 1: 0}
    rim = {-1: 1, 0: pl.ds(1, 2), 1: 2}

    def spectrum_copy(number):
        dr, dc = WAYS[number]
        return remote(part.at[span[dr], span[dc]], got.at[back[dr], back[dc]], number, peer(dr, dc))

    def gradient_copy(number):
        dr, dc = WAYS[number]
        return remote(
            gspec.at[rim[dr], rim[dc]], gspec.at[back[dr], back[dc]], 8 + number, peer(dr, dc)
        )

    target_copy = remote(
        target.at[0, pl.ds(TILE, TILE), pl.ds(TILE, TILE)], tgt.at[4], 16, partner
    )
    share_copy = remote(spec.at[3], spec.at[4], 17, partner)
    result_copy = remote(shared, gspec.at[2, 2], 18, partner)

    for dr, dc in WAYS:

        @pl.when(jnp.logical_not(has(dr, dc)))
        def _():
            rows = 2 if dr == 0 else 1
            cols = 2 if dc == 0 else 1
            for i in range(rows):
                for j in range(cols):
                    a = {-1: 0, 0: 1 + i, 1: 3}[dr]
                    e = {-1: 0, 0: 1 + j, 1: 3}[dc]
                    got[a, e] = jnp.zeros((KF, 2 * KF), BF16)

    loads[0].wait()
    for r in range(4):
        rows = pl.ds(r * 128, 128)
        pixels[rows, :] = jnp.tanh(0.5 * levels[rows, :]).astype(BF16)

    pl.semaphore_wait(barrier, greeted)

    @pl.when(heavy)
    def _():
        target_copy.start()

    loads[1].wait()

    @pl.loop(0, 4)
    def _(r):
        rows = pl.ds(pl.multiple_of(r * 128, 128), 128)
        x = pixels[rows, :]
        halves[rows, 0:128] = dot(x[:, 0:128], edge_v[0:128, 0:128]).astype(BF16)
        halves[rows, 128:384] = dot(x, edge_v[:, 128:384]).astype(BF16)
        halves[rows, 384:512] = dot(x[:, 384:512], edge_v[384:512, 384:512]).astype(BF16)

    loads[2].wait()
    low = low_half((KF, 2 * KF))
    tall = {0: slice(0, 128), 1: slice(0, 384), 2: slice(128, 512), 3: slice(384, 512)}
    for a in (0, 3, 1, 2):
        prod = dot(edge_tv[a * 128 : (a + 1) * 128, tall[a]], halves[tall[a], :])
        for e in range(4):
            top = prod[:KF, e * 128 : (e + 1) * 128]
            low_rows = pltpu.roll(prod[KF:, e * 128 : (e + 1) * 128], KF, 1)
            value = jnp.where(low, top - low_rows, -(top + low_rows))
            if a in (1, 2) and e in (1, 2):
                acc[(a - 1) * 2 + e - 1] = value
            else:
                part[a, e] = value.astype(BF16)

    for number, (dr, dc) in enumerate(WAYS):

        @pl.when(has(dr, dc))
        def _():
            spectrum_copy(number).start()

    loads[3].wait()

    @pl.loop(0, CONDS)
    def _(c):
        for n in range(NK):
            k = kraw[c, n]
            amount = jnp.sqrt(jnp.full((1, 2 * KF), weights[c, n], F32)) * SCALE
            k = k * amount
            turned = pltpu.roll(k, KF, 1)
            kre[c, n * KF : (n + 1) * KF, :] = jnp.where(low, k, turned)
            kim[c, n * KF : (n + 1) * KF, :] = jnp.where(low, -turned, k)

    for load in loads[4:]:
        load.wait()

    for number, (dr, dc) in enumerate(WAYS):

        @pl.when(has(-dr, -dc))
        def _():
            spectrum_copy(number).wait_recv()

    for a in (1, 0):
        for e in (1, 0):
            oa = 3 * a
            oe = 3 * e
            total = (
                acc[a * 2 + e]
                + got[1 + a, oe].astype(F32)
                + got[oa, 1 + e].astype(F32)
                + got[oa, oe].astype(F32)
            )
            spec[a * 2 + e] = total.astype(BF16)
            acc[a * 2 + e] = jnp.zeros((KF, 2 * KF), F32)

        if a == 1:

            @pl.when(heavy)
            def _():
                share_copy.start()

    acc[4] = jnp.zeros((KF, 2 * KF), F32)

    t1 = unit_v.at[0:128, :]
    t2t = unit_v.at[128:256, :]
    upt = unit_v.at[256:384, :]
    up2 = unit_v.at[384:640, :]
    upt3 = unit_v.at[640:1024, :]
    t2 = unit_v.at[1024:1280, 0:128]
    t1t = unit_v.at[1024:1280, 128:256]
    up_lo = unit_v.at[1280:1536, 0:128]
    up = unit_v.at[1280:1536, 128:256]

    def forward(slot, tile, cond):
        s = spec[tile].astype(F32)
        turned = pltpu.roll(s, KF, 1)
        s2 = jnp.concatenate([s, s], 0)
        r2 = jnp.concatenate([turned, turned], 0)
        intensity = None
        for j in range(NK // 2):
            rows = slice(j * 128, (j + 1) * 128)
            mixed = (kre[cond, rows, :] * s2 + kim[cond, rows, :] * r2).astype(BF16)
            row_half = dot(mixed, t1[...]).astype(BF16)
            field = dot(t2[...], swap_pair(row_half))
            fields[slot, j] = field.astype(BF16)
            square = field * field
            square = square[:128] + square[128:]
            square = square[:, :128] + square[:, 128:]
            intensity = square if intensity is None else intensity + square
        return intensity

    def middle(intensity, tile, cond, live):
        hi = intensity.astype(BF16)
        lo = (intensity - hi.astype(F32)).astype(BF16)
        cols = dot(up2[...], jnp.concatenate([hi, lo], 0)) + dot(up_lo[...], hi)
        hi = cols.astype(BF16)
        lo = (cols - hi.astype(F32)).astype(BF16)
        full = dot(jnp.concatenate([hi, lo, hi], 1), upt3[...])
        tau = jnp.tanh((0.5 * STEEPNESS) * (full - thresholds[cond]))
        grad_int = 4.0 * (1.0 + tau - 2.0 * tgt[tile].astype(F32)) * (1.0 - tau * tau)
        down = dot(upt[...], grad_int.astype(BF16)).astype(BF16)
        coarse = dot(down, up[...])
        return jnp.where(live, coarse, 0.0)

    def backward(slot, coarse, tile, cond):
        wide = jnp.concatenate([coarse, coarse], 1)
        sum_re = None
        for j in range(NK // 2):
            rows = slice(j * 128, (j + 1) * 128)
            field = fields[slot, j].astype(F32)
            grad_field = jnp.concatenate([field[:128] * wide, field[128:] * wide], 0).astype(BF16)
            grad_half = dot(t2t[...], grad_field).astype(BF16)
            grad_mix = dot(swap_pair(grad_half), t1t[...])
            term_re = kre[cond, rows, :] * grad_mix
            term_im = kim[cond, rows, :] * grad_mix
            sum_re = term_re if sum_re is None else sum_re + term_re
            sum_im = term_im if j == 0 else sum_im + term_im
        total = sum_re[:KF] + sum_re[KF:] + pltpu.roll(sum_im[:KF] + sum_im[KF:], KF, 1)
        acc[tile] = acc[tile] + total

    def pick(test, a, b):
        return jnp.where(test, a, b).astype(jnp.int32)

    def unit_pair(i, carry):
        @pl.when(jnp.logical_not(heavy) & (i == 1))
        def _():
            target_copy.wait_recv()
            share_copy.wait_recv()

        outer = (i == 0) | (i == 3)
        first = pick(i == 0, 0, 2)
        tiles = [
            pick(heavy, i // 2, pick(outer, first, 4)),
            pick(heavy, i // 2, pick(outer, first + 1, 4)),
        ]
        low_cond = pick(heavy, (i % 2) * 2, pick(outer, 0, (i - 1) * 2))
        conds = [low_cond, pick(heavy, low_cond + 1, pick(outer, 0, low_cond + 1))]
        lives = [
            cond < counts[pick(tile == 4, partner, me), pick(tile == 4, 3, tile)]
            for tile, cond in zip(tiles, conds)
        ]
        sums = [forward(u, tiles[u], conds[u]) for u in range(2)]
        coarse = [middle(sums[u], tiles[u], conds[u], lives[u]) for u in range(2)]
        for u in range(2):
            backward(u, coarse[u], tiles[u], conds[u])

        @pl.when(jnp.logical_not(heavy) & (i == 2))
        def _():
            shared[...] = acc[4].astype(BF16)
            result_copy.start()

        return carry

    lax.fori_loop(0, jnp.where(heavy, 6, 4), unit_pair, jnp.int32(0))

    for k in range(3):
        gspec[1 + k // 2, 1 + k % 2] = acc[k].astype(BF16)

    @pl.when(jnp.logical_not(heavy))
    def _():
        gspec[2, 2] = acc[3].astype(BF16)
        result_copy.wait_send()

    @pl.when(heavy)
    def _():
        result_copy.wait_recv()
        share_copy.wait_send()
        target_copy.wait_send()

    for number, (dr, dc) in enumerate(WAYS):

        @pl.when(has(dr, dc))
        def _():
            spectrum_copy(number).wait_send()
            gradient_copy(number).start()

    for dr, dc in WAYS:

        @pl.when(jnp.logical_not(has(dr, dc)))
        def _():
            rows = 2 if dr == 0 else 1
            cols = 2 if dc == 0 else 1
            for i in range(rows):
                for j in range(cols):
                    a = {-1: 0, 0: 1 + i, 1: 3}[dr]
                    e = {-1: 0, 0: 1 + j, 1: 3}[dc]
                    gspec[a, e] = jnp.zeros((KF, 2 * KF), BF16)

    for number, (dr, dc) in enumerate(WAYS):

        @pl.when(has(dr, dc))
        def _():
            gradient_copy(number).wait_send()

        @pl.when(has(-dr, -dc))
        def _():
            gradient_copy(number).wait_recv()

    out[...] = gspec[...]


def adjoint_kernel(gspec, mask, edge, edge_t, levels_out, gradient_out, whole):
    r = pl.program_id(0)

    @pl.when(r == 0)
    def _():
        low = low_half((KF, 2 * KF))
        for a in range(4):
            for e in range(4):
                g = gspec[a, e].astype(F32)
                cols = slice(e * 128, (e + 1) * 128)
                whole[a * 128 : a * 128 + KF, cols] = jnp.where(low, g, -g).astype(BF16)
                whole[a * 128 + KF : (a + 1) * 128, cols] = (-pltpu.roll(g, KF, 1)).astype(BF16)

    start = pl.multiple_of(((r + 1) // 2) * 128, 128)
    halves = dot(edge[:, pl.ds(start, 256)], whole[pl.ds(start, 256), :]).astype(BF16)
    for cols, rows in (
        (slice(0, 128), slice(0, 256)),
        (slice(128, 384), slice(128, 384)),
        (slice(384, 512), slice(256, 512)),
    ):
        canvas = dot(halves[:, rows], edge_t[rows, cols])
        levels = mask[0, :, cols]
        transmit = jnp.tanh(0.5 * levels)
        gradient = canvas * (0.5 - 0.5 * transmit * transmit)
        gradient_out[0, :, cols] = gradient
        levels_out[0, :, cols] = levels - STEP_SIZE * gradient


def shards(mask_param, target, counts, kernels, weights, thresholds):
    edge = jnp.asarray(EDGE)
    edge_t = jnp.asarray(EDGE_T)
    unit = jnp.asarray(UNIT)
    any_space = pl.BlockSpec(memory_space=pl.ANY)
    smem = pl.BlockSpec(memory_space=pltpu.SMEM)
    block = (KF, 2 * KF)
    gspec = pl.pallas_call(
        gradient_kernel,
        out_shape=jax.ShapeDtypeStruct((4, 4) + block, BF16),
        in_specs=[smem] * 3 + [any_space] * 6,
        out_specs=pl.BlockSpec(memory_space=pltpu.VMEM),
        scratch_shapes=[
            pltpu.VMEM((512, 512), F32),
            pltpu.VMEM((512, 512), BF16),
            pltpu.VMEM((512, 512), BF16),
            pltpu.VMEM((4, 4) + block, BF16),
            pltpu.VMEM((4, 4) + block, BF16),
            pltpu.VMEM((5,) + block, BF16),
            pltpu.VMEM((5, TILE, TILE), BF16),
            pltpu.VMEM((CONDS, NK) + block, F32),
            pltpu.VMEM((CONDS, NK * KF, 2 * KF), F32),
            pltpu.VMEM((CONDS, NK * KF, 2 * KF), F32),
            pltpu.VMEM((2, NK // 2, 256, 256), BF16),
            pltpu.VMEM((5,) + block, F32),
            pltpu.VMEM((4, 4) + block, BF16),
            pltpu.VMEM(block, BF16),
            pltpu.VMEM((512, 512), BF16),
            pltpu.VMEM((512, 512), BF16),
            pltpu.VMEM(UNIT.shape, BF16),
            pltpu.SemaphoreType.DMA((9,)),
            pltpu.SemaphoreType.DMA((19,)),
            pltpu.SemaphoreType.DMA((19,)),
        ],
        compiler_params=pltpu.CompilerParams(
            collective_id=0, has_side_effects=True, vmem_limit_bytes=48 * 1024 * 1024
        ),
        name="gradient",
    )(counts, weights, thresholds, mask_param, target, kernels, edge, edge_t, unit)
    rows = pl.BlockSpec((1, 128, 512), lambda r: (0, r, 0))
    return pl.pallas_call(
        adjoint_kernel,
        grid=(4,),
        out_shape=(
            jax.ShapeDtypeStruct((1, 512, 512), F32),
            jax.ShapeDtypeStruct((1, 512, 512), F32),
        ),
        in_specs=[
            pl.BlockSpec((4, 4) + block, lambda r: (0, 0, 0, 0)),
            rows,
            pl.BlockSpec((128, 512), lambda r: (r, 0)),
            pl.BlockSpec((512, 512), lambda r: (0, 0)),
        ],
        out_specs=(rows, rows),
        scratch_shapes=[pltpu.VMEM((512, 512), BF16)],
        name="adjoint",
    )(gspec, mask_param, edge, edge_t)


def solution(mesh):
    placed = (P("tiles", None, None), P("tiles", None, None), P(), P(), P(), P())
    return jax.shard_map(
        shards,
        mesh=mesh,
        in_specs=placed,
        out_specs=(P("tiles", None, None), P("tiles", None, None)),
        check_vma=False,
    )
```

time: 311 us -> 53.9 us (0.17)
  the two profiles are of different devices: /device:TPU:7 before, /device:TPU:11 now
where the time goes in v1:
time: 53.9 us; the launch traced here: 53.5 us
  Pallas kernels  43.1 us (80%)
  local copies, waits for them, and re-layouts  9.69 us (18%)
  between operations  0.66 us (1%)
    pallas_call x1, Pallas kernels, shards(): pl.pallas_call(gradient_kernel, out_shape=jax.ShapeDtypeStruct((4, 4) + b...  38.4 us
    unnamed x19, local copies, waits for them, and re-layouts  9.69 us
    pallas_call x1, Pallas kernels, shards(): pl.pallas_call(adjoint_kernel, grid=(4,), out_shape=(jax.ShapeDtypeStruct...  4.7 us

profile of v1, /device:TPU:11, one launch (start us, length us, event | category | flops | bytes accessed | tf_op | source)
XLA Modules:
  0.0 53.5 jit_solution(14591997529595464848)
XLA Ops:
  0.6 0.8 %copy.11.counts = s32[128,4]{1,0:T(8,128)S(1)} copy(s32[128,4]{0,1:T(4,128)} %param.11) | data formatting | bytes 4096 | tf_op args[2]
  1.4 0.0 copy-start
  1.4 1.2 %copy-done = f32[1,512,512]{2,1,0:T(8,128)S(1)} copy-done((f32[1,512,512]{2,1,0:T(8,128)S(1)}, f32[1,512,512]{2,1,0:T(8,128)}, u32[]{:S(2)}) %copy-start) | copy-done | bytes 1048600
  2.6 0.0 copy-start.1
  2.6 1.0 %copy-done.1 = bf16[512,512]{1,0:T(8,128)(2,1)S(1)} copy-done((bf16[512,512]{1,0:T(8,128)(2,1)S(1)}, bf16[512,512]{1,0:T(8,128)(2,1)}, u32[]{:S(2)}) %copy-start.1) | copy-done | bytes 524312
  3.7 0.0 copy-start.2
  3.7 1.0 %copy-done.2 = bf16[512,512]{1,0:T(8,128)(2,1)S(1)} copy-done((bf16[512,512]{1,0:T(8,128)(2,1)S(1)}, bf16[512,512]{1,0:T(8,128)(2,1)}, u32[]{:S(2)}) %copy-start.2) | copy-done | bytes 524312
  4.7 0.0 copy-start.3
  4.7 1.4 %copy-done.3 = f32[4,12,64,128]{3,2,1,0:T(8,128)S(1)} copy-done((f32[4,12,64,128]{3,2,1,0:T(8,128)S(1)}, f32[4,12,64,128]{3,2,1,0:T(8,128)}, u32[]{:S(2)}) %copy-start.3) | copy-done | bytes 1572888
  6.1 0.0 copy-start.5
  6.1 1.1 %copy-done.5 = bf16[1536,256]{1,0:T(8,128)(2,1)S(1)} copy-done((bf16[1536,256]{1,0:T(8,128)(2,1)S(1)}, bf16[1536,256]{1,0:T(8,128)(2,1)}, u32[]{:S(2)}) %copy-start.5) | copy-done | bytes 786456
  7.3 0.0 copy-start.6
  7.3 1.0 %copy-done.6 = bf16[1,512,512]{2,1,0:T(8,128)(2,1)S(1)} copy-done((bf16[1,512,512]{2,1,0:T(8,128)(2,1)S(1)}, bf16[1,512,512]{2,1,0:T(8,128)(2,1)}, u32[]{:S(2)}) %copy-start.6) | copy-done | bytes 524312
  8.3 0.0 copy-start.7
  8.3 0.7 %copy-done.7 = f32[4,12]{1,0:T(4,128)S(1)} copy-done((f32[4,12]{1,0:T(4,128)S(1)}, f32[4,12]{1,0:T(4,128)}, u32[]{:S(2)}) %copy-start.7) | copy-done | bytes 216
  9.0 0.0 copy-start.8
  9.0 0.7 %copy-done.8 = f32[4]{0:T(128)S(1)} copy-done((f32[4]{0:T(128)S(1)}, f32[4]{0:T(128)}, u32[]{:S(2)}) %copy-start.8) | copy-done | bytes 40
  9.6 38.4 %gradient.1.gspec = bf16[4,4,64,128]{3,2,1,0:T(8,128)(2,1)S(1)} custom-call(s32[128,4]{1,0:T(8,128)S(1)} %copy.11.counts, f32[4,12]{1,0:T(4,128)S(1)} %copy-done.7, f32[4]{0:T(128)S(1)} %copy-done.8, f32[1,512,512]{2,1,0:T(8,128)S(1)} %copy-done, bf16[1,512,512]{2,1,0:T(8,128)(2,1)S(1)} %copy-done.6, f32[4,12,64,128]{3,2,1,0:T(8,128)S(1)} %copy-done.3, ...), custom_call_target="tpu_custom_call" | custom-call | tf_op jit(solution)/shard_map/gradient/pallas_call | solution.py:447
  48.1 0.0 copy-start.4
  48.1 0.7 %copy-done.4 = bf16[4,4,64,128]{3,2,1,0:T(8,128)(2,1)} copy-done((bf16[4,4,64,128]{3,2,1,0:T(8,128)(2,1)}, bf16[4,4,64,128]{3,2,1,0:T(8,128)(2,1)S(1)}, u32[]{:S(2)}) %copy-start.4) | copy-done | bytes 262168
  48.8 4.7 %adjoint.1 = (f32[1,512,512]{2,1,0:T(8,128)}, f32[1,512,512]{2,1,0:T(8,128)}) custom-call(bf16[4,4,64,128]{3,2,1,0:T(8,128)(2,1)} %copy-done.4, f32[1,512,512]{2,1,0:T(8,128)} %mask.3, bf16[512,512]{1,0:T(8,128)(2,1)} %constant.6.clone.edge, bf16[512,512]{1,0:T(8,128)(2,1)} %constant.7.clone.edge_t), custom_call_target="tpu_custom_call" | custom-call | tf_op jit(solution)/shard_map/adjoint/pallas_call | solution.py:480
Async XLA Ops:
  1.4 1.2 %copy-start = (f32[1,512,512]{2,1,0:T(8,128)S(1)}, f32[1,512,512]{2,1,0:T(8,128)}, u32[]{:S(2)}) copy-start(f32[1,512,512]{2,1,0:T(8,128)} %mask.3) | copy-start | bytes 3145732
  2.6 1.0 %copy-start.1 = (bf16[512,512]{1,0:T(8,128)(2,1)S(1)}, bf16[512,512]{1,0:T(8,128)(2,1)}, u32[]{:S(2)}) copy-start(bf16[512,512]{1,0:T(8,128)(2,1)} %constant.7.clone.edge_t) | copy-start | bytes 1572868
  3.7 1.0 %copy-start.2 = (bf16[512,512]{1,0:T(8,128)(2,1)S(1)}, bf16[512,512]{1,0:T(8,128)(2,1)}, u32[]{:S(2)}) copy-start(bf16[512,512]{1,0:T(8,128)(2,1)} %constant.6.clone.edge) | copy-start | bytes 1572868
  4.7 1.4 %copy-start.3 = (f32[4,12,64,128]{3,2,1,0:T(8,128)S(1)}, f32[4,12,64,128]{3,2,1,0:T(8,128)}, u32[]{:S(2)}) copy-start(f32[4,12,64,128]{3,2,1,0:T(8,128)} %kernels.1) | copy-start | bytes 4718596
  6.1 1.1 %copy-start.5 = (bf16[1536,256]{1,0:T(8,128)(2,1)S(1)}, bf16[1536,256]{1,0:T(8,128)(2,1)}, u32[]{:S(2)}) copy-start(bf16[1536,256]{1,0:T(8,128)(2,1)} %constant.8.clone.unit) | copy-start | bytes 2359300
  7.3 1.0 %copy-start.6 = (bf16[1,512,512]{2,1,0:T(8,128)(2,1)S(1)}, bf16[1,512,512]{2,1,0:T(8,128)(2,1)}, u32[]{:S(2)}) copy-start(bf16[1,512,512]{2,1,0:T(8,128)(2,1)} %target.1) | copy-start | bytes 1572868
  8.3 0.7 %copy-start.7 = (f32[4,12]{1,0:T(4,128)S(1)}, f32[4,12]{1,0:T(4,128)}, u32[]{:S(2)}) copy-start(f32[4,12]{1,0:T(4,128)} %weights.1) | copy-start | bytes 580
  9.0 0.7 %copy-start.8 = (f32[4]{0:T(128)S(1)}, f32[4]{0:T(128)}, u32[]{:S(2)}) copy-start(f32[4]{0:T(128)} %thresholds.1) | copy-start | bytes 52
  48.1 0.7 %copy-start.4 = (bf16[4,4,64,128]{3,2,1,0:T(8,128)(2,1)}, bf16[4,4,64,128]{3,2,1,0:T(8,128)(2,1)S(1)}, u32[]{:S(2)}) copy-start(bf16[4,4,64,128]{3,2,1,0:T(8,128)(2,1)S(1)} %gradient.1.gspec) | copy-start | bytes 786436

commit v2 on v1

--- a/solution.py
+++ b/solution.py
@@ -96,9 +96,9 @@
 
 
 def gradient_kernel(
-    counts, weights, thresholds, mask, target, kernels, edge, edge_t, unit,
+    counts_in, weights_in, thresholds_in, mask, target, kernels, edge, edge_t, unit,
     out,
-    levels, pixels, halves, part, got, spec, tgt, kraw, kre, kim, fields, acc, gspec, shared, edge_v, edge_tv, unit_v,
+    levels, pixels, halves, part, got, spec, tgt, kraw, kre, kim, fields, acc, gspec, shared, edge_v, edge_tv, unit_v, counts, weights, thresholds,
     load_sem, send_sem, recv_sem,
 ):
     me = lax.axis_index("tiles")
@@ -124,6 +124,9 @@
         pltpu.make_async_copy(edge_t, edge_tv, load_sem.at[2]),
         pltpu.make_async_copy(kernels, kraw, load_sem.at[3]),
         pltpu.make_async_copy(unit, unit_v, load_sem.at[4]),
+        pltpu.make_async_copy(counts_in, counts, load_sem.at[9]),
+        pltpu.make_async_copy(thresholds_in, thresholds, load_sem.at[10]),
+        pltpu.make_async_copy(weights_in, weights, load_sem.at[11]),
     ] + [
         pltpu.make_async_copy(
             target.at[0, pl.ds((k // 2) * TILE, TILE), pl.ds((k % 2) * TILE, TILE)],
@@ -230,6 +233,7 @@
             spectrum_copy(number).start()
 
     loads[3].wait()
+    loads[7].wait()
 
     @pl.loop(0, CONDS)
     def _(c):
@@ -241,7 +245,7 @@
             kre[c, n * KF : (n + 1) * KF, :] = jnp.where(low, k, turned)
             kim[c, n * KF : (n + 1) * KF, :] = jnp.where(low, -turned, k)
 
-    for load in loads[4:]:
+    for load in loads[4:7] + loads[8:]:
         load.wait()
 
     for number, (dr, dc) in enumerate(WAYS):
@@ -346,7 +350,7 @@
         low_cond = pick(heavy, (i % 2) * 2, pick(outer, 0, (i - 1) * 2))
         conds = [low_cond, pick(heavy, low_cond + 1, pick(outer, 0, low_cond + 1))]
         lives = [
-            cond < counts[pick(tile == 4, partner, me), pick(tile == 4, 3, tile)]
+            cond < counts[pick(tile == 4, 3, tile), pick(tile == 4, partner, me)]
             for tile, cond in zip(tiles, conds)
         ]
         sums = [forward(u, tiles[u], conds[u]) for u in range(2)]
@@ -441,13 +445,12 @@
     edge = jnp.asarray(EDGE)
     edge_t = jnp.asarray(EDGE_T)
     unit = jnp.asarray(UNIT)
-    any_space = pl.BlockSpec(memory_space=pl.ANY)
-    smem = pl.BlockSpec(memory_space=pltpu.SMEM)
+    any_space = pl.BlockSpec(memory_space=pltpu.HBM)
     block = (KF, 2 * KF)
     gspec = pl.pallas_call(
         gradient_kernel,
         out_shape=jax.ShapeDtypeStruct((4, 4) + block, BF16),
-        in_specs=[smem] * 3 + [any_space] * 6,
+        in_specs=[any_space] * 9,
         out_specs=pl.BlockSpec(memory_space=pltpu.VMEM),
         scratch_shapes=[
             pltpu.VMEM((512, 512), F32),
@@ -467,15 +470,18 @@
             pltpu.VMEM((512, 512), BF16),
             pltpu.VMEM((512, 512), BF16),
             pltpu.VMEM(UNIT.shape, BF16),
-            pltpu.SemaphoreType.DMA((9,)),
+            pltpu.SMEM((4, 128), jnp.int32),
+            pltpu.SMEM((CONDS, NK), F32),
+            pltpu.SMEM((CONDS,), F32),
+            pltpu.SemaphoreType.DMA((12,)),
             pltpu.SemaphoreType.DMA((19,)),
             pltpu.SemaphoreType.DMA((19,)),
         ],
         compiler_params=pltpu.CompilerParams(
-            collective_id=0, has_side_effects=True, vmem_limit_bytes=48 * 1024 * 1024
+            collective_id=0, has_side_effects=True, vmem_limit_bytes=67043328
         ),
         name="gradient",
-    )(counts, weights, thresholds, mask_param, target, kernels, edge, edge_t, unit)
+    )(counts.T, weights, thresholds, mask_param, target, kernels, edge, edge_t, unit)
     rows = pl.BlockSpec((1, 128, 512), lambda r: (0, r, 0))
     return pl.pallas_call(
         adjoint_kernel,

time: 53.9 us -> 42.8 us (0.79)
  local copies, waits for them, and re-layouts: 9.69 us -> 0 us
  Pallas kernels: 43.1 us -> 41.9 us
    unnamed x19 -> x0, local copies, waits for them, and re-layouts: 9.69 us -> none
    pallas_call x1, Pallas kernels: 38.4 us -> 37.2 us  [shards(): pl.pallas_call(gradient_kernel, out_shape=jax.ShapeDtypeStruct((4, 4) + b...]
where the time goes in v2:
time: 42.8 us; the launch traced here: 42.6 us
  Pallas kernels  41.9 us (98%)
  between operations  0.64 us (1%)
    pallas_call x1, Pallas kernels, shards(): pl.pallas_call(gradient_kernel, out_shape=jax.ShapeDtypeStruct((4, 4) + b...  37.2 us
    pallas_call x1, Pallas kernels, shards(): pl.pallas_call(adjoint_kernel, grid=(4,), out_shape=(jax.ShapeDtypeStruct...  4.73 us

profile of v2, /device:TPU:11, one launch (start us, length us, event | category | flops | bytes accessed | tf_op | source)
XLA Modules:
  0.0 42.6 jit_solution(17637143312800543933)
XLA Ops:
  0.6 37.2 %gradient.1.gspec = bf16[4,4,64,128]{3,2,1,0:T(8,128)(2,1)} custom-call(s32[4,128]{1,0:T(4,128)} %bitcast.1, f32[4,12]{1,0:T(4,128)} %weights_in.1, f32[4]{0:T(128)} %thresholds_in.1, f32[1,512,512]{2,1,0:T(8,128)} %mask.3, bf16[1,512,512]{2,1,0:T(8,128)(2,1)} %target.1, f32[4,12,64,128]{3,2,1,0:T(8,128)} %kernels.1, bf16[512,512]{1,0:T(8,128)(2,1)} %constant.6.clone.edge, ...), custom_call_target="tpu_custom_call" | custom-call | tf_op jit(solution)/shard_map/gradient/pallas_call | solution.py:450
  37.8 4.7 %adjoint.1 = (f32[1,512,512]{2,1,0:T(8,128)}, f32[1,512,512]{2,1,0:T(8,128)}) custom-call(bf16[4,4,64,128]{3,2,1,0:T(8,128)(2,1)} %gradient.1.gspec, f32[1,512,512]{2,1,0:T(8,128)} %mask.3, bf16[512,512]{1,0:T(8,128)(2,1)} %constant.6.clone.edge, bf16[512,512]{1,0:T(8,128)(2,1)} %constant.7.clone.edge_t), custom_call_target="tpu_custom_call" | custom-call | tf_op jit(solution)/shard_map/adjoint/pallas_call | solution.py:486

commit v3 on v2

--- a/solution.py
+++ b/solution.py
@@ -63,10 +63,9 @@
             bf(t1),
             bf(t2.T),
             up_hi.T,
-            np.concatenate([up_hi, up_hi], 1),
-            np.concatenate([up_hi.T, up_hi.T, up_lo.T], 0),
+            np.concatenate([up_hi, up_lo], 1),
+            np.concatenate([up_hi.T, up_lo.T], 0),
             np.concatenate([bf(t2), bf(t1.T)], 1),
-            np.concatenate([up_lo, up_hi], 1),
         ],
         0,
     )
@@ -98,7 +97,7 @@
 def gradient_kernel(
     counts_in, weights_in, thresholds_in, mask, target, kernels, edge, edge_t, unit,
     out,
-    levels, pixels, halves, part, got, spec, tgt, kraw, kre, kim, fields, acc, gspec, shared, edge_v, edge_tv, unit_v, counts, weights, thresholds,
+    levels, pixels, halves, part, got, spec, tgt, kraw, kre, kim, row_halves, fields, acc, gspec, shared, edge_v, edge_tv, unit_v, counts, weights, thresholds,
     load_sem, send_sem, recv_sem,
 ):
     me = lax.axis_index("tiles")
@@ -279,55 +278,60 @@
     t2t = unit_v.at[128:256, :]
     upt = unit_v.at[256:384, :]
     up2 = unit_v.at[384:640, :]
-    upt3 = unit_v.at[640:1024, :]
-    t2 = unit_v.at[1024:1280, 0:128]
-    t1t = unit_v.at[1024:1280, 128:256]
-    up_lo = unit_v.at[1280:1536, 0:128]
-    up = unit_v.at[1280:1536, 128:256]
-
-    def forward(slot, tile, cond):
+    upt2 = unit_v.at[640:896, :]
+    t2 = unit_v.at[896:1152, 0:128]
+    t1t = unit_v.at[896:1152, 128:256]
+    up = unit_v.at[384:640, 0:128]
+
+    def mix(slot, tile, cond):
         s = spec[tile].astype(F32)
         turned = pltpu.roll(s, KF, 1)
         s2 = jnp.concatenate([s, s], 0)
         r2 = jnp.concatenate([turned, turned], 0)
-        intensity = None
         for j in range(NK // 2):
             rows = slice(j * 128, (j + 1) * 128)
             mixed = (kre[cond, rows, :] * s2 + kim[cond, rows, :] * r2).astype(BF16)
-            row_half = dot(mixed, t1[...]).astype(BF16)
-            field = dot(t2[...], swap_pair(row_half))
-            fields[slot, j] = field.astype(BF16)
-            square = field * field
-            square = square[:128] + square[128:]
-            square = square[:, :128] + square[:, 128:]
-            intensity = square if intensity is None else intensity + square
-        return intensity
-
-    def middle(intensity, tile, cond, live):
+            row_halves[slot, j] = swap_pair(dot(mixed, t1[...]).astype(BF16))
+
+    def field(slot, j, intensity):
+        value = dot(t2[...], row_halves[slot, j])
+        fields[slot, j] = value.astype(BF16)
+        square = value * value
+        square = square[:128] + square[128:]
+        square = square[:, :128] + square[:, 128:]
+        return square if intensity is None else intensity + square
+
+    def interpolate_rows(intensity):
         hi = intensity.astype(BF16)
-        lo = (intensity - hi.astype(F32)).astype(BF16)
-        cols = dot(up2[...], jnp.concatenate([hi, lo], 0)) + dot(up_lo[...], hi)
+        return dot(up2[...], jnp.concatenate([hi, hi], 0))
+
+    def resist_gradient(cols, tile, cond):
         hi = cols.astype(BF16)
-        lo = (cols - hi.astype(F32)).astype(BF16)
-        full = dot(jnp.concatenate([hi, lo, hi], 1), upt3[...])
+        full = dot(jnp.concatenate([hi, hi], 1), upt2[...])
         tau = jnp.tanh((0.5 * STEEPNESS) * (full - thresholds[cond]))
         grad_int = 4.0 * (1.0 + tau - 2.0 * tgt[tile].astype(F32)) * (1.0 - tau * tau)
-        down = dot(upt[...], grad_int.astype(BF16)).astype(BF16)
-        coarse = dot(down, up[...])
-        return jnp.where(live, coarse, 0.0)
-
-    def backward(slot, coarse, tile, cond):
+        return grad_int.astype(BF16)
+
+    def coarse_rows(grad_int):
+        return dot(upt[...], grad_int).astype(BF16)
+
+    def coarse_gradient(down, live):
+        return jnp.where(live, dot(down, up[...]), 0.0).astype(BF16)
+
+    def grad_halves(slot, j, coarse):
         wide = jnp.concatenate([coarse, coarse], 1)
+        value = fields[slot, j]
+        grad_field = jnp.concatenate([value[:128] * wide, value[128:] * wide], 0)
+        row_halves[slot, j] = swap_pair(dot(t2t[...], grad_field).astype(BF16))
+
+    def gather(slot, tile, cond):
         sum_re = None
         for j in range(NK // 2):
             rows = slice(j * 128, (j + 1) * 128)
-            field = fields[slot, j].astype(F32)
-            grad_field = jnp.concatenate([field[:128] * wide, field[128:] * wide], 0).astype(BF16)
-            grad_half = dot(t2t[...], grad_field).astype(BF16)
-            grad_mix = dot(swap_pair(grad_half), t1t[...])
+            grad_mix = dot(row_halves[slot, j], t1t[...])
             term_re = kre[cond, rows, :] * grad_mix
             term_im = kim[cond, rows, :] * grad_mix
-            sum_re = term_re if sum_re is None else sum_re + term_re
+            sum_re = term_re if j == 0 else sum_re + term_re
             sum_im = term_im if j == 0 else sum_im + term_im
         total = sum_re[:KF] + sum_re[KF:] + pltpu.roll(sum_im[:KF] + sum_im[KF:], KF, 1)
         acc[tile] = acc[tile] + total
@@ -353,10 +357,35 @@
             cond < counts[pick(tile == 4, 3, tile), pick(tile == 4, partner, me)]
             for tile, cond in zip(tiles, conds)
         ]
-        sums = [forward(u, tiles[u], conds[u]) for u in range(2)]
-        coarse = [middle(sums[u], tiles[u], conds[u], lives[u]) for u in range(2)]
         for u in range(2):
-            backward(u, coarse[u], tiles[u], conds[u])
+            mix(u, tiles[u], conds[u])
+        bright = [None, None]
+        for j in range(6):
+            bright[0] = field(0, j, bright[0])
+        for j in range(2):
+            bright[1] = field(1, j, bright[1])
+        cols = interpolate_rows(bright[0])
+        bright[1] = field(1, 2, bright[1])
+        grad_int = resist_gradient(cols, tiles[0], conds[0])
+        bright[1] = field(1, 3, bright[1])
+        bright[1] = field(1, 4, bright[1])
+        down = coarse_rows(grad_int)
+        bright[1] = field(1, 5, bright[1])
+        coarse = coarse_gradient(down, lives[0])
+        cols = interpolate_rows(bright[1])
+        for j in range(2):
+            grad_halves(0, j, coarse)
+        grad_int = resist_gradient(cols, tiles[1], conds[1])
+        for j in range(2, 4):
+            grad_halves(0, j, coarse)
+        down = coarse_rows(grad_int)
+        for j in range(4, 6):
+            grad_halves(0, j, coarse)
+        coarse = coarse_gradient(down, lives[1])
+        gather(0, tiles[0], conds[0])
+        for j in range(6):
+            grad_halves(1, j, coarse)
+        gather(1, tiles[1], conds[1])
 
         @pl.when(jnp.logical_not(heavy) & (i == 2))
         def _():
@@ -463,6 +492,7 @@
             pltpu.VMEM((CONDS, NK) + block, F32),
             pltpu.VMEM((CONDS, NK * KF, 2 * KF), F32),
             pltpu.VMEM((CONDS, NK * KF, 2 * KF), F32),
+            pltpu.VMEM((2, NK // 2, 128, 256), BF16),
             pltpu.VMEM((2, NK // 2, 256, 256), BF16),
             pltpu.VMEM((5,) + block, F32),
             pltpu.VMEM((4, 4) + block, BF16),

time: 42.8 us -> 36.2 us (0.85)
  Pallas kernels: 41.9 us -> 35.4 us
    pallas_call x1, Pallas kernels: 37.2 us -> 30.7 us  [shards(): pl.pallas_call(gradient_kernel, out_shape=jax.ShapeDtypeStruct((4, 4) + b...]
where the time goes in v3:
time: 36.2 us; the launch traced here: 36 us
  Pallas kernels  35.4 us (98%)
  between operations  0.64 us (2%)
    pallas_call x1, Pallas kernels, shards(): pl.pallas_call(gradient_kernel, out_shape=jax.ShapeDtypeStruct((4, 4) + b...  30.7 us
    pallas_call x1, Pallas kernels, shards(): pl.pallas_call(adjoint_kernel, grid=(4,), out_shape=(jax.ShapeDtypeStruct...  4.73 us

profile of v3, /device:TPU:11, one launch (start us, length us, event | category | flops | bytes accessed | tf_op | source)
XLA Modules:
  0.0 36.0 jit_solution(17220273513317418871)
XLA Ops:
  0.6 30.7 %gradient.1.gspec = bf16[4,4,64,128]{3,2,1,0:T(8,128)(2,1)} custom-call(s32[4,128]{1,0:T(4,128)} %bitcast.1, f32[4,12]{1,0:T(4,128)} %weights_in.1, f32[4]{0:T(128)} %thresholds_in.1, f32[1,512,512]{2,1,0:T(8,128)} %mask.3, bf16[1,512,512]{2,1,0:T(8,128)(2,1)} %target.1, f32[4,12,64,128]{3,2,1,0:T(8,128)} %kernels.1, bf16[512,512]{1,0:T(8,128)(2,1)} %constant.6.clone.edge, ...), custom_call_target="tpu_custom_call" | custom-call | tf_op jit(solution)/shard_map/gradient/pallas_call | solution.py:479
  31.3 4.7 %adjoint.1 = (f32[1,512,512]{2,1,0:T(8,128)}, f32[1,512,512]{2,1,0:T(8,128)}) custom-call(bf16[4,4,64,128]{3,2,1,0:T(8,128)(2,1)} %gradient.1.gspec, f32[1,512,512]{2,1,0:T(8,128)} %mask.3, bf16[512,512]{1,0:T(8,128)(2,1)} %constant.6.clone.edge, bf16[512,512]{1,0:T(8,128)(2,1)} %constant.7.clone.edge_t), custom_call_target="tpu_custom_call" | custom-call | tf_op jit(solution)/shard_map/adjoint/pallas_call | solution.py:516

commit v4 on v3

--- a/solution.py
+++ b/solution.py
@@ -17,6 +17,7 @@
 COARSE = 2 * KF
 NK = 12
 CONDS = 4
+UNITS = 4
 STEEPNESS = 8.0
 STEP_SIZE = 0.25
 SCALE = 1.0 / (PADDED * KF)
@@ -339,62 +340,63 @@
     def pick(test, a, b):
         return jnp.where(test, a, b).astype(jnp.int32)
 
-    def unit_pair(i, carry):
+    def unit_group(i, carry):
         @pl.when(jnp.logical_not(heavy) & (i == 1))
         def _():
             target_copy.wait_recv()
             share_copy.wait_recv()
 
-        outer = (i == 0) | (i == 3)
-        first = pick(i == 0, 0, 2)
-        tiles = [
-            pick(heavy, i // 2, pick(outer, first, 4)),
-            pick(heavy, i // 2, pick(outer, first + 1, 4)),
-        ]
-        low_cond = pick(heavy, (i % 2) * 2, pick(outer, 0, (i - 1) * 2))
-        conds = [low_cond, pick(heavy, low_cond + 1, pick(outer, 0, low_cond + 1))]
+        own = jnp.logical_not(heavy) & (i == 0)
+        tile = pick(heavy, i, 4)
+        tiles = [pick(own, u, tile) for u in range(UNITS)]
+        conds = [pick(own, 0, u) for u in range(UNITS)]
         lives = [
             cond < counts[pick(tile == 4, 3, tile), pick(tile == 4, partner, me)]
             for tile, cond in zip(tiles, conds)
         ]
-        for u in range(2):
-            mix(u, tiles[u], conds[u])
-        bright = [None, None]
+        args = list(zip(tiles, conds))
+        bright = [None] * UNITS
+        coarse = [None] * UNITS
+
+        def fields_step(u, j):
+            bright[u] = field(u, j, bright[u])
+
+        def halves_step(u, j):
+            grad_halves(u, j, coarse[u])
+
+        def middle_between(u, steps):
+            cols = interpolate_rows(bright[u])
+            for step in steps[:2]:
+                step()
+            grad_int = resist_gradient(cols, *args[u])
+            for step in steps[2:4]:
+                step()
+            down = coarse_rows(grad_int)
+            for step in steps[4:]:
+                step()
+            coarse[u] = coarse_gradient(down, lives[u])
+
+        for u in range(UNITS):
+            mix(u, *args[u])
         for j in range(6):
-            bright[0] = field(0, j, bright[0])
-        for j in range(2):
-            bright[1] = field(1, j, bright[1])
-        cols = interpolate_rows(bright[0])
-        bright[1] = field(1, 2, bright[1])
-        grad_int = resist_gradient(cols, tiles[0], conds[0])
-        bright[1] = field(1, 3, bright[1])
-        bright[1] = field(1, 4, bright[1])
-        down = coarse_rows(grad_int)
-        bright[1] = field(1, 5, bright[1])
-        coarse = coarse_gradient(down, lives[0])
-        cols = interpolate_rows(bright[1])
-        for j in range(2):
-            grad_halves(0, j, coarse)
-        grad_int = resist_gradient(cols, tiles[1], conds[1])
-        for j in range(2, 4):
-            grad_halves(0, j, coarse)
-        down = coarse_rows(grad_int)
-        for j in range(4, 6):
-            grad_halves(0, j, coarse)
-        coarse = coarse_gradient(down, lives[1])
-        gather(0, tiles[0], conds[0])
-        for j in range(6):
-            grad_halves(1, j, coarse)
-        gather(1, tiles[1], conds[1])
-
-        @pl.when(jnp.logical_not(heavy) & (i == 2))
+            fields_step(0, j)
+        for u in range(UNITS - 1):
+            middle_between(u, [functools.partial(fields_step, u + 1, j) for j in range(6)])
+        middle_between(UNITS - 1, [functools.partial(halves_step, 0, j) for j in range(6)])
+        for u in range(1, UNITS):
+            for j in range(6):
+                halves_step(u, j)
+            gather(u - 1, *args[u - 1])
+        gather(UNITS - 1, *args[UNITS - 1])
+
+        @pl.when(jnp.logical_not(heavy) & (i == 1))
         def _():
             shared[...] = acc[4].astype(BF16)
             result_copy.start()
 
         return carry
 
-    lax.fori_loop(0, jnp.where(heavy, 6, 4), unit_pair, jnp.int32(0))
+    lax.fori_loop(0, jnp.where(heavy, 3, 2), unit_group, jnp.int32(0))
 
     for k in range(3):
         gspec[1 + k // 2, 1 + k % 2] = acc[k].astype(BF16)
@@ -442,32 +444,40 @@
     out[...] = gspec[...]
 
 
-def adjoint_kernel(gspec, mask, edge, edge_t, levels_out, gradient_out, whole):
-    r = pl.program_id(0)
-
-    @pl.when(r == 0)
-    def _():
-        low = low_half((KF, 2 * KF))
-        for a in range(4):
-            for e in range(4):
-                g = gspec[a, e].astype(F32)
-                cols = slice(e * 128, (e + 1) * 128)
-                whole[a * 128 : a * 128 + KF, cols] = jnp.where(low, g, -g).astype(BF16)
-                whole[a * 128 + KF : (a + 1) * 128, cols] = (-pltpu.roll(g, KF, 1)).astype(BF16)
-
-    start = pl.multiple_of(((r + 1) // 2) * 128, 128)
-    halves = dot(edge[:, pl.ds(start, 256)], whole[pl.ds(start, 256), :]).astype(BF16)
-    for cols, rows in (
-        (slice(0, 128), slice(0, 256)),
-        (slice(128, 384), slice(128, 384)),
-        (slice(384, 512), slice(256, 512)),
-    ):
-        canvas = dot(halves[:, rows], edge_t[rows, cols])
-        levels = mask[0, :, cols]
-        transmit = jnp.tanh(0.5 * levels)
-        gradient = canvas * (0.5 - 0.5 * transmit * transmit)
-        gradient_out[0, :, cols] = gradient
-        levels_out[0, :, cols] = levels - STEP_SIZE * gradient
+def adjoint_kernel(gspec, mask, edge, edge_t, levels_out, gradient_out, whole, levels, gradient, sem):
+    low = low_half((KF, 2 * KF))
+
+    def unfold(a):
+        for e in range(4):
+            g = gspec[a, e].astype(F32)
+            cols = slice(e * 128, (e + 1) * 128)
+            whole[a * 128 : a * 128 + KF, cols] = jnp.where(low, g, -g).astype(BF16)
+            whole[a * 128 + KF : (a + 1) * 128, cols] = (-pltpu.roll(g, KF, 1)).astype(BF16)
+
+    copies = []
+    for r in range(4):
+        for a in {0: (0, 1), 1: (2,), 2: (), 3: (3,)}[r]:
+            unfold(a)
+        rows = slice(r * 128, (r + 1) * 128)
+        start = ((r + 1) // 2) * 128
+        halves = dot(edge[rows, start : start + 256], whole[start : start + 256, :]).astype(BF16)
+        for cols, tall in (
+            (slice(0, 128), slice(0, 256)),
+            (slice(128, 384), slice(128, 384)),
+            (slice(384, 512), slice(256, 512)),
+        ):
+            canvas = dot(halves[:, tall], edge_t[tall, cols])
+            before = mask[0, rows, cols]
+            transmit = jnp.tanh(0.5 * before)
+            grad = canvas * (0.5 - 0.5 * transmit * transmit)
+            gradient[rows, cols] = grad
+            levels[rows, cols] = before - STEP_SIZE * grad
+        for k, (source, out) in enumerate(((gradient, gradient_out), (levels, levels_out))):
+            copy = pltpu.make_async_copy(source.at[rows], out.at[0, rows], sem.at[k, r])
+            copy.start()
+            copies.append(copy)
+    for copy in copies:
+        copy.wait()
 
 
 def shards(mask_param, target, counts, kernels, weights, thresholds):
@@ -492,8 +502,8 @@
             pltpu.VMEM((CONDS, NK) + block, F32),
             pltpu.VMEM((CONDS, NK * KF, 2 * KF), F32),
             pltpu.VMEM((CONDS, NK * KF, 2 * KF), F32),
-            pltpu.VMEM((2, NK // 2, 128, 256), BF16),
-            pltpu.VMEM((2, NK // 2, 256, 256), BF16),
+            pltpu.VMEM((UNITS, NK // 2, 128, 256), BF16),
+            pltpu.VMEM((UNITS, NK // 2, 256, 256), BF16),
             pltpu.VMEM((5,) + block, F32),
             pltpu.VMEM((4, 4) + block, BF16),
             pltpu.VMEM(block, BF16),
@@ -508,26 +518,24 @@
             pltpu.SemaphoreType.DMA((19,)),
         ],
         compiler_params=pltpu.CompilerParams(
-            collective_id=0, has_side_effects=True, vmem_limit_bytes=67043328
+            collective_id=0, has_side_effects=True, vmem_limit_bytes=67043328 - 4 * 1024 * 1024
         ),
         name="gradient",
     )(counts.T, weights, thresholds, mask_param, target, kernels, edge, edge_t, unit)
-    rows = pl.BlockSpec((1, 128, 512), lambda r: (0, r, 0))
+    vmem = pl.BlockSpec(memory_space=pltpu.VMEM)
+    plane = jax.ShapeDtypeStruct((1, 512, 512), F32)
     return pl.pallas_call(
         adjoint_kernel,
-        grid=(4,),
-        out_shape=(
-            jax.ShapeDtypeStruct((1, 512, 512), F32),
-            jax.ShapeDtypeStruct((1, 512, 512), F32),
-        ),
-        in_specs=[
-            pl.BlockSpec((4, 4) + block, lambda r: (0, 0, 0, 0)),
-            rows,
-            pl.BlockSpec((128, 512), lambda r: (r, 0)),
-            pl.BlockSpec((512, 512), lambda r: (0, 0)),
+        out_shape=(plane, plane),
+        in_specs=[vmem] * 4,
+        out_specs=(any_space, any_space),
+        scratch_shapes=[
+            pltpu.VMEM((512, 512), BF16),
+            pltpu.VMEM((512, 512), F32),
+            pltpu.VMEM((512, 512), F32),
+            pltpu.SemaphoreType.DMA((2, 4)),
         ],
-        out_specs=(rows, rows),
-        scratch_shapes=[pltpu.VMEM((512, 512), BF16)],
+        compiler_params=pltpu.CompilerParams(vmem_limit_bytes=16 * 1024 * 1024),
         name="adjoint",
     )(gspec, mask_param, edge, edge_t)
 

time: 36.2 us -> 32.6 us (0.901)
  Pallas kernels: 35.4 us -> 30.8 us
  local copies, waits for them, and re-layouts: 0 us -> 0.96 us
    pallas_call x1, Pallas kernels: 4.73 us -> 1.87 us  [shards(): pl.pallas_call(adjoint_kernel, out_shape=(plane, plane), in_specs=[vmem]...]
    pallas_call x1, Pallas kernels: 30.7 us -> 28.9 us  [shards(): pl.pallas_call(gradient_kernel, out_shape=jax.ShapeDtypeStruct((4, 4) + b...]
    unnamed x0 -> x8, local copies, waits for them, and re-layouts: none -> 0.96 us
where the time goes in v4:
time: 32.6 us; the launch traced here: 32.4 us
  Pallas kernels  30.8 us (94%)
  local copies, waits for them, and re-layouts  0.96 us (3%)
  between operations  0.7 us (2%)
    pallas_call x1, Pallas kernels, shards(): pl.pallas_call(gradient_kernel, out_shape=jax.ShapeDtypeStruct((4, 4) + b...  28.9 us
    pallas_call x1, Pallas kernels, shards(): pl.pallas_call(adjoint_kernel, out_shape=(plane, plane), in_specs=[vmem]...  1.87 us
    unnamed x8, local copies, waits for them, and re-layouts  0.96 us

profile of v4, /device:TPU:11, one launch (start us, length us, event | category | flops | bytes accessed | tf_op | source)
XLA Modules:
  0.0 32.4 jit_solution(14957462522518315178)
XLA Ops:
  0.6 0.0 copy-start
  0.6 0.0 copy-start.1
  0.7 0.0 copy-start.2
  0.7 28.9 %gradient.1.gspec = bf16[4,4,64,128]{3,2,1,0:T(8,128)(2,1)} custom-call(s32[4,128]{1,0:T(4,128)} %bitcast.1, f32[4,12]{1,0:T(4,128)} %weights_in.1, f32[4]{0:T(128)} %thresholds_in.1, f32[1,512,512]{2,1,0:T(8,128)} %mask.3, bf16[1,512,512]{2,1,0:T(8,128)(2,1)} %target.1, f32[4,12,64,128]{3,2,1,0:T(8,128)} %kernels.1, bf16[512,512]{1,0:T(8,128)(2,1)} %constant.6.clone.edge, ...), custom_call_target="tpu_custom_call" | custom-call | tf_op jit(solution)/shard_map/gradient/pallas_call | solution.py:489
  29.6 0.0 copy-done
  29.6 0.0 copy-done.1
  29.6 0.0 copy-done.2
  29.6 0.0 copy-start.3
  29.6 0.9 %copy-done.3 = bf16[4,4,64,128]{3,2,1,0:T(8,128)(2,1)S(1)} copy-done((bf16[4,4,64,128]{3,2,1,0:T(8,128)(2,1)S(1)}, bf16[4,4,64,128]{3,2,1,0:T(8,128)(2,1)}, u32[]{:S(2)}) %copy-start.3) | copy-done | bytes 262168
  30.6 1.9 %adjoint.1 = (f32[1,512,512]{2,1,0:T(8,128)}, f32[1,512,512]{2,1,0:T(8,128)}) custom-call(bf16[4,4,64,128]{3,2,1,0:T(8,128)(2,1)S(1)} %copy-done.3, f32[1,512,512]{2,1,0:T(8,128)S(1)} %copy-done, bf16[512,512]{1,0:T(8,128)(2,1)S(1)} %copy-done.2, bf16[512,512]{1,0:T(8,128)(2,1)S(1)} %copy-done.1), custom_call_target="tpu_custom_call" | custom-call | tf_op jit(solution)/shard_map/adjoint/pallas_call | solution.py:527
Async XLA Ops:
  0.6 29.0 %copy-start = (f32[1,512,512]{2,1,0:T(8,128)S(1)}, f32[1,512,512]{2,1,0:T(8,128)}, u32[]{:S(2)}) copy-start(f32[1,512,512]{2,1,0:T(8,128)} %mask.3) | copy-start | bytes 3145732
  0.6 29.0 %copy-start.1 = (bf16[512,512]{1,0:T(8,128)(2,1)S(1)}, bf16[512,512]{1,0:T(8,128)(2,1)}, u32[]{:S(2)}) copy-start(bf16[512,512]{1,0:T(8,128)(2,1)} %constant.7.clone.edge_t) | copy-start | bytes 1572868
  0.7 29.0 %copy-start.2 = (bf16[512,512]{1,0:T(8,128)(2,1)S(1)}, bf16[512,512]{1,0:T(8,128)(2,1)}, u32[]{:S(2)}) copy-start(bf16[512,512]{1,0:T(8,128)(2,1)} %constant.6.clone.edge) | copy-start | bytes 1572868
  29.6 1.0 %copy-start.3 = (bf16[4,4,64,128]{3,2,1,0:T(8,128)(2,1)S(1)}, bf16[4,4,64,128]{3,2,1,0:T(8,128)(2,1)}, u32[]{:S(2)}) copy-start(bf16[4,4,64,128]{3,2,1,0:T(8,128)(2,1)} %gradient.1.gspec) | copy-start | bytes 786436

commit v5 on v4

--- a/solution.py
+++ b/solution.py
@@ -72,6 +72,39 @@
     )
 
 
+STAGES = (
+    ("mix", 1, 123, 150),
+    ("field", NK // 2, 53, 250),
+    ("rows", 1, 70, 250),
+    ("resist", 1, 70, 400),
+    ("down", 1, 53, 200),
+    ("coarse", 1, 53, 250),
+    ("half", NK // 2, 53, 200),
+    ("gather", 1, 141, 0),
+)
+
+
+def unit_order(units):
+    at = [[0, 0, 0.0] for _ in range(units)]
+    clock, order = 0.0, []
+    while any(stage < len(STAGES) for stage, _, _ in at):
+        alive = [u for u in range(units) if at[u][0] < len(STAGES)]
+        u = next((u for u in alive if at[u][2] <= clock), None)
+        if u is None:
+            clock = min(at[u][2] for u in alive)
+            continue
+        stage, j, _ = at[u]
+        name, steps, length, wait = STAGES[stage]
+        order.append((u, name, j))
+        clock += length
+        if j + 1 < steps:
+            at[u][1] = j + 1
+        else:
+            at[u] = [stage + 1, 0, clock + wait]
+    return order
+
+
+ORDER = unit_order(UNITS)
 EDGE = edge_table()
 EDGE_T = np.ascontiguousarray(EDGE.T)
 UNIT = unit_tables()
@@ -98,7 +131,7 @@
 def gradient_kernel(
     counts_in, weights_in, thresholds_in, mask, target, kernels, edge, edge_t, unit,
     out,
-    levels, pixels, halves, part, got, spec, tgt, kraw, kre, kim, row_halves, fields, acc, gspec, shared, edge_v, edge_tv, unit_v, counts, weights, thresholds,
+    levels, halves, part, got, spec, tgt, kraw, kre, kim, row_halves, fields, acc, gspec, shared, edge_v, edge_tv, unit_v, counts, weights, thresholds,
     load_sem, send_sem, recv_sem,
 ):
     me = lax.axis_index("tiles")
@@ -118,8 +151,15 @@
     def peer(dr, dc):
         return lax.rem(me + dr * DEV_COLS + dc + devices, devices)
 
+    order = (0, 3, 1, 2)
+    first_loads = [
+        pltpu.make_async_copy(
+            mask.at[0, pl.ds(r * 128, 128)], levels.at[pl.ds(r * 128, 128)], load_sem.at[12 + r]
+        )
+        for r in range(4)
+    ]
     loads = [
-        pltpu.make_async_copy(mask.at[0], levels, load_sem.at[0]),
+        None,
         pltpu.make_async_copy(edge, edge_v, load_sem.at[1]),
         pltpu.make_async_copy(edge_t, edge_tv, load_sem.at[2]),
         pltpu.make_async_copy(kernels, kraw, load_sem.at[3]),
@@ -135,8 +175,12 @@
         )
         for k in range(4)
     ]
-    for load in loads:
-        load.start()
+    first_loads[0].start()
+    first_loads[3].start()
+    loads[1].start()
+    first_loads[1].start()
+    first_loads[2].start()
+    loads[2].start()
 
     barrier = pltpu.get_barrier_semaphore()
     greeted = jnp.int32(1)
@@ -167,17 +211,28 @@
         dr, dc = WAYS[number]
         return remote(part.at[span[dr], span[dc]], got.at[back[dr], back[dc]], number, peer(dr, dc))
 
-    def gradient_copy(number):
-        dr, dc = WAYS[number]
-        return remote(
-            gspec.at[rim[dr], rim[dc]], gspec.at[back[dr], back[dc]], 8 + number, peer(dr, dc)
-        )
+    def gradient_copies(k):
+        a, e = k // 2, k % 2
+        dr, dc = 2 * a - 1, 2 * e - 1
+        ways = ((dr, 0), (0, dc), (dr, dc))
+        slots = ((back[dr], 1 + e), (1 + a, back[dc]), (back[dr], back[dc]))
+        return [
+            (way, remote(gspec.at[1 + a, 1 + e], gspec.at[slot], 9 + 3 * k + n, peer(*way)))
+            for n, (way, slot) in enumerate(zip(ways, slots))
+        ]
+
+    def publish(k):
+        for way, copy in gradient_copies(k):
+
+            @pl.when(has(*way))
+            def _():
+                copy.start()
 
     target_copy = remote(
-        target.at[0, pl.ds(TILE, TILE), pl.ds(TILE, TILE)], tgt.at[4], 16, partner
+        target.at[0, pl.ds(TILE, TILE), pl.ds(TILE, TILE)], tgt.at[4], 21, partner
     )
-    share_copy = remote(spec.at[3], spec.at[4], 17, partner)
-    result_copy = remote(shared, gspec.at[2, 2], 18, partner)
+    share_copy = remote(spec.at[3], spec.at[4], 8, partner)
+    result_copy = remote(shared, gspec.at[2, 2], 22, partner)
 
     for dr, dc in WAYS:
 
@@ -190,32 +245,12 @@
                     a = {-1: 0, 0: 1 + i, 1: 3}[dr]
                     e = {-1: 0, 0: 1 + j, 1: 3}[dc]
                     got[a, e] = jnp.zeros((KF, 2 * KF), BF16)
-
-    loads[0].wait()
-    for r in range(4):
-        rows = pl.ds(r * 128, 128)
-        pixels[rows, :] = jnp.tanh(0.5 * levels[rows, :]).astype(BF16)
-
-    pl.semaphore_wait(barrier, greeted)
-
-    @pl.when(heavy)
-    def _():
-        target_copy.start()
-
-    loads[1].wait()
-
-    @pl.loop(0, 4)
-    def _(r):
-        rows = pl.ds(pl.multiple_of(r * 128, 128), 128)
-        x = pixels[rows, :]
-        halves[rows, 0:128] = dot(x[:, 0:128], edge_v[0:128, 0:128]).astype(BF16)
-        halves[rows, 128:384] = dot(x, edge_v[:, 128:384]).astype(BF16)
-        halves[rows, 384:512] = dot(x[:, 384:512], edge_v[384:512, 384:512]).astype(BF16)
-
-    loads[2].wait()
+                    gspec[a, e] = jnp.zeros((KF, 2 * KF), BF16)
+
     low = low_half((KF, 2 * KF))
     tall = {0: slice(0, 128), 1: slice(0, 384), 2: slice(128, 512), 3: slice(384, 512)}
-    for a in (0, 3, 1, 2):
+
+    def products(a):
         prod = dot(edge_tv[a * 128 : (a + 1) * 128, tall[a]], halves[tall[a], :])
         for e in range(4):
             top = prod[:KF, e * 128 : (e + 1) * 128]
@@ -226,11 +261,36 @@
             else:
                 part[a, e] = value.astype(BF16)
 
-    for number, (dr, dc) in enumerate(WAYS):
-
-        @pl.when(has(dr, dc))
-        def _():
-            spectrum_copy(number).start()
+    def send_spectra(step):
+        for number, (dr, dc) in enumerate(WAYS):
+            if dr == step:
+
+                @pl.when(has(dr, dc))
+                def _():
+                    spectrum_copy(number).start()
+
+    for r in order:
+        rows = slice(r * 128, (r + 1) * 128)
+        first_loads[r].wait()
+        x = jnp.tanh(0.5 * levels[rows, :]).astype(BF16)
+        if r == 0:
+            loads[1].wait()
+        halves[rows, 0:128] = dot(x[:, 0:128], edge_v[0:128, 0:128]).astype(BF16)
+        halves[rows, 128:384] = dot(x, edge_v[:, 128:384]).astype(BF16)
+        halves[rows, 384:512] = dot(x[:, 384:512], edge_v[384:512, 384:512]).astype(BF16)
+        if r == 0:
+            loads[2].wait()
+            for load in loads[3:]:
+                load.start()
+            products(0)
+            pl.semaphore_wait(barrier, greeted)
+            send_spectra(-1)
+        if r == 3:
+            products(3)
+            send_spectra(1)
+    products(1)
+    products(2)
+    send_spectra(0)
 
     loads[3].wait()
     loads[7].wait()
@@ -271,6 +331,7 @@
 
             @pl.when(heavy)
             def _():
+                target_copy.start()
                 share_copy.start()
 
     acc[4] = jnp.zeros((KF, 2 * KF), F32)
@@ -355,91 +416,73 @@
             for tile, cond in zip(tiles, conds)
         ]
         args = list(zip(tiles, conds))
-        bright = [None] * UNITS
-        coarse = [None] * UNITS
-
-        def fields_step(u, j):
-            bright[u] = field(u, j, bright[u])
-
-        def halves_step(u, j):
-            grad_halves(u, j, coarse[u])
-
-        def middle_between(u, steps):
-            cols = interpolate_rows(bright[u])
-            for step in steps[:2]:
-                step()
-            grad_int = resist_gradient(cols, *args[u])
-            for step in steps[2:4]:
-                step()
-            down = coarse_rows(grad_int)
-            for step in steps[4:]:
-                step()
-            coarse[u] = coarse_gradient(down, lives[u])
-
-        for u in range(UNITS):
-            mix(u, *args[u])
-        for j in range(6):
-            fields_step(0, j)
-        for u in range(UNITS - 1):
-            middle_between(u, [functools.partial(fields_step, u + 1, j) for j in range(6)])
-        middle_between(UNITS - 1, [functools.partial(halves_step, 0, j) for j in range(6)])
-        for u in range(1, UNITS):
-            for j in range(6):
-                halves_step(u, j)
-            gather(u - 1, *args[u - 1])
-        gather(UNITS - 1, *args[UNITS - 1])
+        state = [{"bright": None} for _ in range(UNITS)]
+
+        def emit(u, stage, j):
+            now = state[u]
+            if stage == "mix":
+                mix(u, *args[u])
+            elif stage == "field":
+                now["bright"] = field(u, j, now["bright"])
+            elif stage == "rows":
+                now["cols"] = interpolate_rows(now["bright"])
+            elif stage == "resist":
+                now["grad"] = resist_gradient(now["cols"], *args[u])
+            elif stage == "down":
+                now["down"] = coarse_rows(now["grad"])
+            elif stage == "coarse":
+                now["coarse"] = coarse_gradient(now["down"], lives[u])
+            elif stage == "half":
+                grad_halves(u, j, now["coarse"])
+            else:
+                gather(u, *args[u])
+
+        for step in ORDER:
+            emit(*step)
 
         @pl.when(jnp.logical_not(heavy) & (i == 1))
         def _():
             shared[...] = acc[4].astype(BF16)
             result_copy.start()
 
+        for k in range(4):
+
+            @pl.when(pick(heavy, pick(i == k, 1, 0) * (1 if k < 3 else 0), pick(i == 0, 1, 0)) == 1)
+            def _():
+                gspec[1 + k // 2, 1 + k % 2] = acc[k].astype(BF16)
+                publish(k)
+
         return carry
 
     lax.fori_loop(0, jnp.where(heavy, 3, 2), unit_group, jnp.int32(0))
-
-    for k in range(3):
-        gspec[1 + k // 2, 1 + k % 2] = acc[k].astype(BF16)
-
-    @pl.when(jnp.logical_not(heavy))
-    def _():
-        gspec[2, 2] = acc[3].astype(BF16)
-        result_copy.wait_send()
 
     @pl.when(heavy)
     def _():
         result_copy.wait_recv()
+        publish(3)
         share_copy.wait_send()
         target_copy.wait_send()
+
+    @pl.when(jnp.logical_not(heavy))
+    def _():
+        result_copy.wait_send()
 
     for number, (dr, dc) in enumerate(WAYS):
 
         @pl.when(has(dr, dc))
         def _():
             spectrum_copy(number).wait_send()
-            gradient_copy(number).start()
-
-    for dr, dc in WAYS:
-
-        @pl.when(jnp.logical_not(has(dr, dc)))
-        def _():
-            rows = 2 if dr == 0 else 1
-            cols = 2 if dc == 0 else 1
-            for i in range(rows):
-                for j in range(cols):
-                    a = {-1: 0, 0: 1 + i, 1: 3}[dr]
-                    e = {-1: 0, 0: 1 + j, 1: 3}[dc]
-                    gspec[a, e] = jnp.zeros((KF, 2 * KF), BF16)
-
-    for number, (dr, dc) in enumerate(WAYS):
-
-        @pl.when(has(dr, dc))
-        def _():
-            gradient_copy(number).wait_send()
-
-        @pl.when(has(-dr, -dc))
-        def _():
-            gradient_copy(number).wait_recv()
+
+    for k in range(4):
+        for (dr, dc), copy in gradient_copies(k):
+
+            @pl.when(has(dr, dc))
+            def _():
+                copy.wait_send()
+
+            @pl.when(has(-dr, -dc))
+            def _():
+                copy.wait_recv()
 
     out[...] = gspec[...]
 
@@ -494,7 +537,6 @@
         scratch_shapes=[
             pltpu.VMEM((512, 512), F32),
             pltpu.VMEM((512, 512), BF16),
-            pltpu.VMEM((512, 512), BF16),
             pltpu.VMEM((4, 4) + block, BF16),
             pltpu.VMEM((4, 4) + block, BF16),
             pltpu.VMEM((5,) + block, BF16),
@@ -513,9 +555,9 @@
             pltpu.SMEM((4, 128), jnp.int32),
             pltpu.SMEM((CONDS, NK), F32),
             pltpu.SMEM((CONDS,), F32),
-            pltpu.SemaphoreType.DMA((12,)),
-            pltpu.SemaphoreType.DMA((19,)),
-            pltpu.SemaphoreType.DMA((19,)),
+            pltpu.SemaphoreType.DMA((16,)),
+            pltpu.SemaphoreType.DMA((23,)),
+            pltpu.SemaphoreType.DMA((23,)),
         ],
         compiler_params=pltpu.CompilerParams(
             collective_id=0, has_side_effects=True, vmem_limit_bytes=67043328 - 4 * 1024 * 1024

time: 32.6 us -> 30.8 us (0.945)
  Pallas kernels: 30.8 us -> 28.7 us
    pallas_call x1, Pallas kernels: 28.9 us -> 26.9 us  [shards(): pl.pallas_call(gradient_kernel, out_shape=jax.ShapeDtypeStruct((4, 4) + b...]
where the time goes in v5:
time: 30.8 us; the launch traced here: 30.4 us
  Pallas kernels  28.7 us (93%)
  local copies, waits for them, and re-layouts  0.96 us (3%)
  between operations  0.7 us (2%)
    pallas_call x1, Pallas kernels, shards(): pl.pallas_call(gradient_kernel, out_shape=jax.ShapeDtypeStruct((4, 4) + b...  26.9 us
    pallas_call x1, Pallas kernels, shards(): pl.pallas_call(adjoint_kernel, out_shape=(plane, plane), in_specs=[vmem]...  1.87 us
    unnamed x8, local copies, waits for them, and re-layouts  0.96 us

profile of v5, /device:TPU:11, one launch (start us, length us, event | category | flops | bytes accessed | tf_op | source)
XLA Modules:
  0.0 30.4 jit_solution(9852434798795359404)
XLA Ops:
  0.6 0.0 copy-start
  0.6 0.0 copy-start.1
  0.7 0.0 copy-start.2
  0.7 26.9 %gradient.1.gspec = bf16[4,4,64,128]{3,2,1,0:T(8,128)(2,1)} custom-call(s32[4,128]{1,0:T(4,128)} %bitcast.1, f32[4,12]{1,0:T(4,128)} %weights_in.1, f32[4]{0:T(128)} %thresholds_in.1, f32[1,512,512]{2,1,0:T(8,128)} %mask.3, bf16[1,512,512]{2,1,0:T(8,128)(2,1)} %target.1, f32[4,12,64,128]{3,2,1,0:T(8,128)} %kernels.1, bf16[512,512]{1,0:T(8,128)(2,1)} %constant.6.clone.edge, ...), custom_call_target="tpu_custom_call" | custom-call | tf_op jit(solution)/shard_map/gradient/pallas_call | solution.py:532
  27.5 0.0 copy-done
  27.5 0.0 copy-done.1
  27.5 0.0 copy-done.2
  27.6 0.0 copy-start.3
  27.6 0.9 %copy-done.3 = bf16[4,4,64,128]{3,2,1,0:T(8,128)(2,1)S(1)} copy-done((bf16[4,4,64,128]{3,2,1,0:T(8,128)(2,1)S(1)}, bf16[4,4,64,128]{3,2,1,0:T(8,128)(2,1)}, u32[]{:S(2)}) %copy-start.3) | copy-done | bytes 262168
  28.5 1.9 %adjoint.1 = (f32[1,512,512]{2,1,0:T(8,128)}, f32[1,512,512]{2,1,0:T(8,128)}) custom-call(bf16[4,4,64,128]{3,2,1,0:T(8,128)(2,1)S(1)} %copy-done.3, f32[1,512,512]{2,1,0:T(8,128)S(1)} %copy-done, bf16[512,512]{1,0:T(8,128)(2,1)S(1)} %copy-done.2, bf16[512,512]{1,0:T(8,128)(2,1)S(1)} %copy-done.1), custom_call_target="tpu_custom_call" | custom-call | tf_op jit(solution)/shard_map/adjoint/pallas_call | solution.py:569
Async XLA Ops:
  0.6 26.9 %copy-start = (f32[1,512,512]{2,1,0:T(8,128)S(1)}, f32[1,512,512]{2,1,0:T(8,128)}, u32[]{:S(2)}) copy-start(f32[1,512,512]{2,1,0:T(8,128)} %mask.3) | copy-start | bytes 3145732
  0.6 26.9 %copy-start.1 = (bf16[512,512]{1,0:T(8,128)(2,1)S(1)}, bf16[512,512]{1,0:T(8,128)(2,1)}, u32[]{:S(2)}) copy-start(bf16[512,512]{1,0:T(8,128)(2,1)} %constant.7.clone.edge_t) | copy-start | bytes 1572868
  0.7 26.9 %copy-start.2 = (bf16[512,512]{1,0:T(8,128)(2,1)S(1)}, bf16[512,512]{1,0:T(8,128)(2,1)}, u32[]{:S(2)}) copy-start(bf16[512,512]{1,0:T(8,128)(2,1)} %constant.6.clone.edge) | copy-start | bytes 1572868
  27.6 1.0 %copy-start.3 = (bf16[4,4,64,128]{3,2,1,0:T(8,128)(2,1)S(1)}, bf16[4,4,64,128]{3,2,1,0:T(8,128)(2,1)}, u32[]{:S(2)}) copy-start(bf16[4,4,64,128]{3,2,1,0:T(8,128)(2,1)} %gradient.1.gspec) | copy-start | bytes 786436

commit v6 on v5

--- a/solution.py
+++ b/solution.py
@@ -531,7 +531,7 @@
     block = (KF, 2 * KF)
     gspec = pl.pallas_call(
         gradient_kernel,
-        out_shape=jax.ShapeDtypeStruct((4, 4) + block, BF16),
+        out_shape=pltpu.VMEM((4, 4) + block, BF16),
         in_specs=[any_space] * 9,
         out_specs=pl.BlockSpec(memory_space=pltpu.VMEM),
         scratch_shapes=[
@@ -563,7 +563,7 @@
             collective_id=0, has_side_effects=True, vmem_limit_bytes=67043328 - 4 * 1024 * 1024
         ),
         name="gradient",
-    )(counts.T, weights, thresholds, mask_param, target, kernels, edge, edge_t, unit)
+    )(*[pltpu.with_memory_space_constraint(x, pltpu.HBM) for x in (counts.T, weights, thresholds, mask_param, target, kernels, edge, edge_t, unit)])
     vmem = pl.BlockSpec(memory_space=pltpu.VMEM)
     plane = jax.ShapeDtypeStruct((1, 512, 512), F32)
     return pl.pallas_call(

time: 30.8 us -> 29.2 us (0.948)
  local copies, waits for them, and re-layouts: 0.96 us -> 0.02 us
  Pallas kernels: 28.7 us -> 28 us
    unnamed x8 -> x6, local copies, waits for them, and re-layouts: 0.96 us -> 0.02 us
    pallas_call x1, Pallas kernels: 26.9 us -> 26.2 us  [shards(): pl.pallas_call(gradient_kernel, out_shape=pltpu.VMEM((4, 4) + block, BF16...]
where the time goes in v6:
time: 29.2 us; the launch traced here: 28.7 us
  Pallas kernels  28 us (96%)
  between operations  0.69 us (2%)
    pallas_call x1, Pallas kernels, shards(): pl.pallas_call(gradient_kernel, out_shape=pltpu.VMEM((4, 4) + block, BF16...  26.2 us
    pallas_call x1, Pallas kernels, shards(): pl.pallas_call(adjoint_kernel, out_shape=(plane, plane), in_specs=[vmem]...  1.87 us

profile of v6, /device:TPU:11, one launch (start us, length us, event | category | flops | bytes accessed | tf_op | source)
XLA Modules:
  0.0 28.7 jit_solution(11365492052085552313)
XLA Ops:
  0.6 0.0 copy-start
  0.6 0.0 copy-start.1
  0.7 0.0 copy-start.2
  0.7 26.2 %gradient.1.gspec = bf16[4,4,64,128]{3,2,1,0:T(8,128)(2,1)S(1)} custom-call(s32[4,128]{1,0:T(4,128)} %bitcast.1, f32[4,12]{1,0:T(4,128)} %weights_in.1, f32[4]{0:T(128)} %thresholds_in.1, f32[1,512,512]{2,1,0:T(8,128)} %mask.3, bf16[1,512,512]{2,1,0:T(8,128)(2,1)} %target.1, f32[4,12,64,128]{3,2,1,0:T(8,128)} %kernels.1, ...), custom_call_target="tpu_custom_call" | custom-call | tf_op jit(solution)/shard_map/gradient/pallas_call | solution.py:532
  26.8 0.0 copy-done
  26.8 0.0 copy-done.1
  26.9 0.0 copy-done.2
  26.9 1.9 %adjoint.1 = (f32[1,512,512]{2,1,0:T(8,128)}, f32[1,512,512]{2,1,0:T(8,128)}) custom-call(bf16[4,4,64,128]{3,2,1,0:T(8,128)(2,1)S(1)} %gradient.1.gspec, f32[1,512,512]{2,1,0:T(8,128)S(1)} %copy-done, bf16[512,512]{1,0:T(8,128)(2,1)S(1)} %copy-done.2, bf16[512,512]{1,0:T(8,128)(2,1)S(1)} %copy-done.1), custom_call_target="tpu_custom_call" | custom-call | tf_op jit(solution)/shard_map/adjoint/pallas_call | solution.py:569
Async XLA Ops:
  0.6 26.2 %copy-start = (f32[1,512,512]{2,1,0:T(8,128)S(1)}, f32[1,512,512]{2,1,0:T(8,128)}, u32[]{:S(2)}) copy-start(f32[1,512,512]{2,1,0:T(8,128)} %mask.3) | copy-start | bytes 3145732
  0.6 26.2 %copy-start.1 = (bf16[512,512]{1,0:T(8,128)(2,1)S(1)}, bf16[512,512]{1,0:T(8,128)(2,1)}, u32[]{:S(2)}) copy-start(bf16[512,512]{1,0:T(8,128)(2,1)} %constant.7.clone.edge_t) | copy-start | bytes 1572868
  0.7 26.2 %copy-start.2 = (bf16[512,512]{1,0:T(8,128)(2,1)S(1)}, bf16[512,512]{1,0:T(8,128)(2,1)}, u32[]{:S(2)}) copy-start(bf16[512,512]{1,0:T(8,128)(2,1)} %constant.6.clone.edge) | copy-start | bytes 1572868

commit v7 on v6

--- a/solution.py
+++ b/solution.py
@@ -25,6 +25,7 @@
 F32 = jnp.float32
 BF16 = jnp.bfloat16
 MESH = pl.DeviceIdType.MESH
+BEYOND = ((1, 0), (0, 1), (1, 1))
 WAYS = [(dr, dc) for dr in (-1, 0, 1) for dc in (-1, 0, 1) if (dr, dc) != (0, 0)]
 
 
@@ -142,14 +143,43 @@
     my_row = me // DEV_COLS
     grid_rows = devices // DEV_COLS
     heavy = me < half
-    partner = me + (3 - 2 * (me // quarter)) * quarter
+
+    def partner_of(device):
+        return device + (3 - 2 * (device // quarter)) * quarter
+
+    partner = partner_of(me)
 
     def has(dr, dc):
         ok = (my_row + dr >= 0) & (my_row + dr < grid_rows)
         return ok & (my_col + dc >= 0) & (my_col + dc < DEV_COLS)
 
+    def partner_has(dr, dc):
+        ok = (partner // DEV_COLS + dr < grid_rows) & (partner % DEV_COLS + dc < DEV_COLS)
+        return jnp.logical_not(heavy) & ok
+
     def peer(dr, dc):
         return lax.rem(me + dr * DEV_COLS + dc + devices, devices)
+
+    barrier = pltpu.get_barrier_semaphore()
+    greeted = jnp.int32(1)
+    for dr, dc in WAYS:
+        greeted = greeted + has(dr, dc).astype(jnp.int32)
+
+        @pl.when(has(dr, dc))
+        def _():
+            pl.semaphore_signal(barrier, inc=1, device_id=(peer(dr, dc),), device_id_type=MESH)
+
+    pl.semaphore_signal(barrier, inc=1, device_id=(partner,), device_id_type=MESH)
+    for dr, dc in BEYOND:
+        greeted = greeted + partner_has(dr, dc).astype(jnp.int32)
+        owner = me - dr * DEV_COLS - dc
+
+        @pl.when(has(-dr, -dc) & (owner < half))
+        def _():
+            pl.semaphore_signal(
+                barrier, inc=1, device_id=(partner_of(owner),), device_id_type=MESH
+            )
+
 
     order = (0, 3, 1, 2)
     first_loads = [
@@ -182,17 +212,6 @@
     first_loads[2].start()
     loads[2].start()
 
-    barrier = pltpu.get_barrier_semaphore()
-    greeted = jnp.int32(1)
-    for dr, dc in WAYS:
-        greeted = greeted + has(dr, dc).astype(jnp.int32)
-
-        @pl.when(has(dr, dc))
-        def _():
-            pl.semaphore_signal(barrier, inc=1, device_id=(peer(dr, dc),), device_id_type=MESH)
-
-    pl.semaphore_signal(barrier, inc=1, device_id=(partner,), device_id_type=MESH)
-
     def remote(src, dst, number, to):
         return pltpu.make_async_remote_copy(
             src_ref=src,
@@ -233,19 +252,20 @@
     )
     share_copy = remote(spec.at[3], spec.at[4], 8, partner)
     result_copy = remote(shared, gspec.at[2, 2], 22, partner)
-
-    for dr, dc in WAYS:
-
-        @pl.when(jnp.logical_not(has(dr, dc)))
-        def _():
-            rows = 2 if dr == 0 else 1
-            cols = 2 if dc == 0 else 1
-            for i in range(rows):
-                for j in range(cols):
-                    a = {-1: 0, 0: 1 + i, 1: 3}[dr]
-                    e = {-1: 0, 0: 1 + j, 1: 3}[dc]
-                    got[a, e] = jnp.zeros((KF, 2 * KF), BF16)
-                    gspec[a, e] = jnp.zeros((KF, 2 * KF), BF16)
+    result_copies = [
+        (
+            way,
+            pltpu.make_async_remote_copy(
+                src_ref=shared,
+                dst_ref=gspec.at[slot],
+                send_sem=send_sem.at[23 + n],
+                recv_sem=recv_sem.at[18 + n],
+                device_id=(lax.rem(partner + way[0] * DEV_COLS + way[1], devices),),
+                device_id_type=MESH,
+            ),
+        )
+        for n, (way, slot) in enumerate(zip(BEYOND, ((0, 2), (2, 0), (0, 0))))
+    ]
 
     low = low_half((KF, 2 * KF))
     tall = {0: slice(0, 128), 1: slice(0, 384), 2: slice(128, 512), 3: slice(384, 512)}
@@ -292,6 +312,19 @@
     products(2)
     send_spectra(0)
 
+    for dr, dc in WAYS:
+
+        @pl.when(jnp.logical_not(has(dr, dc)))
+        def _():
+            rows = 2 if dr == 0 else 1
+            cols = 2 if dc == 0 else 1
+            for i in range(rows):
+                for j in range(cols):
+                    a = {-1: 0, 0: 1 + i, 1: 3}[dr]
+                    e = {-1: 0, 0: 1 + j, 1: 3}[dc]
+                    got[a, e] = jnp.zeros((KF, 2 * KF), BF16)
+                    gspec[a, e] = jnp.zeros((KF, 2 * KF), BF16)
+
     loads[3].wait()
     loads[7].wait()
 
@@ -393,10 +426,11 @@
             grad_mix = dot(row_halves[slot, j], t1t[...])
             term_re = kre[cond, rows, :] * grad_mix
             term_im = kim[cond, rows, :] * grad_mix
+            term_re = term_re[:KF] + term_re[KF:]
+            term_im = term_im[:KF] + term_im[KF:]
             sum_re = term_re if j == 0 else sum_re + term_re
             sum_im = term_im if j == 0 else sum_im + term_im
-        total = sum_re[:KF] + sum_re[KF:] + pltpu.roll(sum_im[:KF] + sum_im[KF:], KF, 1)
-        acc[tile] = acc[tile] + total
+        acc[tile] = acc[tile] + (sum_re + pltpu.roll(sum_im, KF, 1))
 
     def pick(test, a, b):
         return jnp.where(test, a, b).astype(jnp.int32)
@@ -444,6 +478,12 @@
         def _():
             shared[...] = acc[4].astype(BF16)
             result_copy.start()
+            for way, copy in result_copies:
+
+                @pl.when(partner_has(*way))
+                def _():
+                    copy.start()
+
 
         for k in range(4):
 
@@ -459,13 +499,18 @@
     @pl.when(heavy)
     def _():
         result_copy.wait_recv()
-        publish(3)
         share_copy.wait_send()
         target_copy.wait_send()
 
     @pl.when(jnp.logical_not(heavy))
     def _():
         result_copy.wait_send()
+        for way, copy in result_copies:
+
+            @pl.when(partner_has(*way))
+            def _():
+                copy.wait_send()
+
 
     for number, (dr, dc) in enumerate(WAYS):
 
@@ -476,7 +521,7 @@
     for k in range(4):
         for (dr, dc), copy in gradient_copies(k):
 
-            @pl.when(has(dr, dc))
+            @pl.when(has(dr, dc) & jnp.logical_not(heavy) if k == 3 else has(dr, dc))
             def _():
                 copy.wait_send()
 
@@ -556,7 +601,7 @@
             pltpu.SMEM((CONDS, NK), F32),
             pltpu.SMEM((CONDS,), F32),
             pltpu.SemaphoreType.DMA((16,)),
-            pltpu.SemaphoreType.DMA((23,)),
+            pltpu.SemaphoreType.DMA((26,)),
             pltpu.SemaphoreType.DMA((23,)),
         ],
         compiler_params=pltpu.CompilerParams(

time: 29.2 us -> 27.2 us (0.932); the launches traced: 28.7 us -> 27.1 us
  Pallas kernels: 28 us -> 26.4 us
    pallas_call x1, Pallas kernels: 26.2 us -> 24.5 us  [shards(): pl.pallas_call(gradient_kernel, out_shape=pltpu.VMEM((4, 4) + block, BF16...]
where the time goes in v7:
time: 27.2 us; the launch traced here: 27.1 us
  Pallas kernels  26.4 us (97%)
  between operations  0.69 us (3%)
    pallas_call x1, Pallas kernels, shards(): pl.pallas_call(gradient_kernel, out_shape=pltpu.VMEM((4, 4) + block, BF16...  24.5 us
    pallas_call x1, Pallas kernels, shards(): pl.pallas_call(adjoint_kernel, out_shape=(plane, plane), in_specs=[vmem]...  1.87 us

profile of v7, /device:TPU:11, one launch (start us, length us, event | category | flops | bytes accessed | tf_op | source)
XLA Modules:
  0.0 27.1 jit_solution(12475009739024660566)
XLA Ops:
  0.6 0.0 copy-start
  0.6 0.0 copy-start.1
  0.7 0.0 copy-start.2
  0.7 24.5 %gradient.1.gspec = bf16[4,4,64,128]{3,2,1,0:T(8,128)(2,1)S(1)} custom-call(s32[4,128]{1,0:T(4,128)} %bitcast.1, f32[4,12]{1,0:T(4,128)} %weights_in.1, f32[4]{0:T(128)} %thresholds_in.1, f32[1,512,512]{2,1,0:T(8,128)} %mask.3, bf16[1,512,512]{2,1,0:T(8,128)(2,1)} %target.1, f32[4,12,64,128]{3,2,1,0:T(8,128)} %kernels.1, ...), custom_call_target="tpu_custom_call" | custom-call | tf_op jit(solution)/shard_map/gradient/pallas_call | solution.py:577
  25.2 0.0 copy-done
  25.2 0.0 copy-done.1
  25.2 0.0 copy-done.2
  25.2 1.9 %adjoint.1 = (f32[1,512,512]{2,1,0:T(8,128)}, f32[1,512,512]{2,1,0:T(8,128)}) custom-call(bf16[4,4,64,128]{3,2,1,0:T(8,128)(2,1)S(1)} %gradient.1.gspec, f32[1,512,512]{2,1,0:T(8,128)S(1)} %copy-done, bf16[512,512]{1,0:T(8,128)(2,1)S(1)} %copy-done.2, bf16[512,512]{1,0:T(8,128)(2,1)S(1)} %copy-done.1), custom_call_target="tpu_custom_call" | custom-call | tf_op jit(solution)/shard_map/adjoint/pallas_call | solution.py:614
Async XLA Ops:
  0.6 24.6 %copy-start = (f32[1,512,512]{2,1,0:T(8,128)S(1)}, f32[1,512,512]{2,1,0:T(8,128)}, u32[]{:S(2)}) copy-start(f32[1,512,512]{2,1,0:T(8,128)} %mask.3) | copy-start | bytes 3145732
  0.6 24.6 %copy-start.1 = (bf16[512,512]{1,0:T(8,128)(2,1)S(1)}, bf16[512,512]{1,0:T(8,128)(2,1)}, u32[]{:S(2)}) copy-start(bf16[512,512]{1,0:T(8,128)(2,1)} %constant.7.clone.edge_t) | copy-start | bytes 1572868
  0.7 24.6 %copy-start.2 = (bf16[512,512]{1,0:T(8,128)(2,1)S(1)}, bf16[512,512]{1,0:T(8,128)(2,1)}, u32[]{:S(2)}) copy-start(bf16[512,512]{1,0:T(8,128)(2,1)} %constant.6.clone.edge) | copy-start | bytes 1572868

commit v8 on v7

--- a/solution.py
+++ b/solution.py
@@ -241,7 +241,7 @@
         ]
 
     def publish(k):
-        for way, copy in gradient_copies(k):
+        for way, copy in reversed(gradient_copies(k)):
 
             @pl.when(has(*way))
             def _():
@@ -282,7 +282,7 @@
                 part[a, e] = value.astype(BF16)
 
     def send_spectra(step):
-        for number, (dr, dc) in enumerate(WAYS):
+        for number, (dr, dc) in sorted(enumerate(WAYS), key=lambda item: item[1][1] == 0):
             if dr == step:
 
                 @pl.when(has(dr, dc))
@@ -512,6 +512,10 @@
                 copy.wait_send()
 
 
+    for a in (1, 2):
+        for e in (1, 2):
+            out[a, e] = gspec[a, e]
+
     for number, (dr, dc) in enumerate(WAYS):
 
         @pl.when(has(dr, dc))
@@ -529,7 +533,11 @@
             def _():
                 copy.wait_recv()
 
-    out[...] = gspec[...]
+    out[0] = gspec[0]
+    out[3] = gspec[3]
+    for a in (1, 2):
+        out[a, 0] = gspec[a, 0]
+        out[a, 3] = gspec[a, 3]
 
 
 def adjoint_kernel(gspec, mask, edge, edge_t, levels_out, gradient_out, whole, levels, gradient, sem):

time: 27.2 us -> 27.4 us (level)
  no operation moved by 1% of the time
where the time goes in v8:
time: 27.4 us; the launch traced here: 27.3 us
  Pallas kernels  26.6 us (97%)
  between operations  0.69 us (3%)
    pallas_call x1, Pallas kernels, shards(): pl.pallas_call(gradient_kernel, out_shape=pltpu.VMEM((4, 4) + block, BF16...  24.7 us
    pallas_call x1, Pallas kernels, shards(): pl.pallas_call(adjoint_kernel, out_shape=(plane, plane), in_specs=[vmem]...  1.87 us

profile of v8, /device:TPU:11, one launch (start us, length us, event | category | flops | bytes accessed | tf_op | source)
XLA Modules:
  0.0 27.3 jit_solution(4405811904108881934)
XLA Ops:
  0.6 0.0 copy-start
  0.6 0.0 copy-start.1
  0.7 0.0 copy-start.2
  0.7 24.7 %gradient.1.gspec = bf16[4,4,64,128]{3,2,1,0:T(8,128)(2,1)S(1)} custom-call(s32[4,128]{1,0:T(4,128)} %bitcast.1, f32[4,12]{1,0:T(4,128)} %weights_in.1, f32[4]{0:T(128)} %thresholds_in.1, f32[1,512,512]{2,1,0:T(8,128)} %mask.3, bf16[1,512,512]{2,1,0:T(8,128)(2,1)} %target.1, f32[4,12,64,128]{3,2,1,0:T(8,128)} %kernels.1, ...), custom_call_target="tpu_custom_call" | custom-call | tf_op jit(solution)/shard_map/gradient/pallas_call | solution.py:585
  25.4 0.0 copy-done
  25.4 0.0 copy-done.1
  25.4 0.0 copy-done.2
  25.4 1.9 %adjoint.1 = (f32[1,512,512]{2,1,0:T(8,128)}, f32[1,512,512]{2,1,0:T(8,128)}) custom-call(bf16[4,4,64,128]{3,2,1,0:T(8,128)(2,1)S(1)} %gradient.1.gspec, f32[1,512,512]{2,1,0:T(8,128)S(1)} %copy-done, bf16[512,512]{1,0:T(8,128)(2,1)S(1)} %copy-done.2, bf16[512,512]{1,0:T(8,128)(2,1)S(1)} %copy-done.1), custom_call_target="tpu_custom_call" | custom-call | tf_op jit(solution)/shard_map/adjoint/pallas_call | solution.py:622
Async XLA Ops:
  0.6 24.7 %copy-start = (f32[1,512,512]{2,1,0:T(8,128)S(1)}, f32[1,512,512]{2,1,0:T(8,128)}, u32[]{:S(2)}) copy-start(f32[1,512,512]{2,1,0:T(8,128)} %mask.3) | copy-start | bytes 3145732
  0.6 24.7 %copy-start.1 = (bf16[512,512]{1,0:T(8,128)(2,1)S(1)}, bf16[512,512]{1,0:T(8,128)(2,1)}, u32[]{:S(2)}) copy-start(bf16[512,512]{1,0:T(8,128)(2,1)} %constant.7.clone.edge_t) | copy-start | bytes 1572868
  0.7 24.7 %copy-start.2 = (bf16[512,512]{1,0:T(8,128)(2,1)S(1)}, bf16[512,512]{1,0:T(8,128)(2,1)}, u32[]{:S(2)}) copy-start(bf16[512,512]{1,0:T(8,128)(2,1)} %constant.6.clone.edge) | copy-start | bytes 1572868
